TPU v7x, 512 devices: a whole 4x4x16 slice. The times are simulated.
512 devices in a mesh: seq: 16 (over z_lo, core), head: 32 (over z_hi, x, y).
Axes of the slice: x: 4, y: 4, z: 16 (z_hi: 2, z_lo: 8; z = z_hi * 8 + z_lo), core: 2. Of those that a mesh axis runs over, the one named last changes fastest.
Arguments:
- queries: bfloat16 [1024, 16384], P('seq', 'head'), may hold values from -8 to 8
- new_keys: bfloat16 [1024, 1024], P('seq'), may hold values from -6 to 6
- new_values: bfloat16 [1024, 1024], P('seq'), may hold values from -6 to 6
- cache_keys: bfloat16 [12288, 1024], P('seq'), may hold values from -8 to 8
- cache_values: bfloat16 [12288, 1024], P('seq'), may hold values from -6 to 6
- positions: int32 [1024], replicated, may hold values from 0 to 1023, each once
- cache_len: int32 [16], replicated, may hold values from 1 to 768, 7680 in all
- out_weight: bfloat16 [16384, 16384], P('head', 'seq'), may hold values from -3.5 to 3.5
Outputs:
- output: float32 [1024, 16384], P(None, 'seq')
Inputs may be any that keep to these rules, and one draw needn't show every extreme that they name: A permutation of the block's positions 0 to 1023. `cache_len`: entry s is the number of live slots at the start of sequence group s's 768 cache slots; later slots of that group are not attended. Some group is full.
All inputs are finite; a program needn't handle non-finite values.
Results may differ from a plain program's by a relative error of at most 0.009.
Values may be sent and summed in bfloat16 or wider, within the bound.
No kernel may reach another device: no remote copies, remote signals or barrier semaphores. Data moves between devices by JAX's collectives and lax.ppermute only.
A program may use at most 128 MiB of HBM per device.

v0:
```python
from functools import partial

import jax
import jax.numpy as jnp
from jax import lax
from jax.sharding import Mesh
from jax.sharding import PartitionSpec as P

DH = 128
GQA = 16
HEAD = ("head_0", "head_1", "head_2")


def sent_to_all(x, axis):
    copies = jnp.broadcast_to(x, (lax.axis_size(axis), *x.shape))
    return lax.all_to_all(copies, axis, split_axis=0, concat_axis=0, tiled=True)


def laid_out(blocks, dim):
    blocks = jnp.moveaxis(blocks, 0, dim)
    shape = blocks.shape
    return blocks.reshape(*shape[:dim], shape[dim] * shape[dim + 1], *shape[dim + 2 :])


def gather_directly(x, axis, dim):
    blocks = sent_to_all(x, axis)
    return laid_out(blocks, dim)


def cut_along(x, dim, size):
    shape = x.shape
    blocks = x.reshape(*shape[:dim], size, shape[dim] // size, *shape[dim + 1 :])
    return jnp.moveaxis(blocks, dim, 0)


def summed_on_arrival(x, axis, dim):
    size = lax.axis_size(axis)
    blocks = lax.all_to_all(cut_along(x, dim, size), axis, 0, 0, tiled=True)
    return jnp.sum(blocks, axis=0)


def sum_in_two_steps(x, axes, dim):
    far, near = axes
    own = summed_on_arrival(cut_along(x, dim, lax.axis_size(far)), near, dim + 1)
    return jnp.sum(lax.all_to_all(own, far, 0, 0, tiled=True), axis=0)


def padded_to(lines, size):
    spare = -lines.shape[0] % size
    if not spare:
        return lines
    return jnp.concatenate([lines, jnp.zeros((spare, *lines.shape[1:]), lines.dtype)])


def gather_axes(x, axes, dim):
    far, near = axes
    blocks = sent_to_all(sent_to_all(x, far), near)
    return laid_out(blocks.swapaxes(0, 1).reshape(-1, *x.shape), dim)


def nested_sum(x, axes):
    lines = x.reshape(-1, x.shape[-1])
    own = sum_in_two_steps(
        padded_to(lines, lax.axis_size(axes[0]) * lax.axis_size(axes[1])), axes, 0
    )
    whole = gather_axes(own, axes, 0)
    return whole[: len(lines)].reshape(x.shape)


def key_mask(count, query_pos, positions, cache_len, stripe, tok_dev):
    index = jnp.arange(count, dtype=jnp.int32)
    span = stripe + tok_dev
    group = index // span
    offset = index % span
    groups = jnp.arange(cache_len.shape[0], dtype=jnp.int32)
    live_len = jnp.sum(jnp.where(group[:, None] == groups[None, :], cache_len[None, :], 0), axis=1)
    is_cache = offset < stripe
    token = jnp.clip(group * tok_dev + offset - stripe, 0, positions.shape[0] - 1)
    key_pos = jnp.take(positions, token)
    return jnp.where(
        is_cache[None, :], (offset < live_len)[None, :], key_pos[None, :] <= query_pos[:, None]
    )


def softmax_step(
    state, block, begin, query_heads, query_pos, positions, cache_len, stripe, tok_dev
):
    running_max, running_sum, weighted = state
    keys = block[:, :DH]
    values = block[:, DH:]
    scores = jnp.einsum(
        "thd,kd->thk", query_heads, keys, preferred_element_type=jnp.float32
    ) * DH ** (-0.5)
    shown = key_mask(block.shape[0], query_pos, positions, cache_len, stripe, tok_dev)[:, None, :]
    scores = jnp.where(shown, scores, -1e30)
    new_max = jnp.maximum(running_max, jnp.max(scores, axis=2))
    expo = jnp.where(shown, jnp.exp(scores - new_max[:, :, None]), 0.0)
    running_sum = jnp.sum(expo, axis=2)
    weighted = jnp.einsum(
        "thk,kd->thd", expo.astype(jnp.bfloat16), values, preferred_element_type=jnp.float32
    )
    return (new_max, running_sum, weighted)


def empty_state(rows, heads_dev):
    return (
        jnp.full((rows, heads_dev), -1e30, jnp.float32),
        jnp.zeros((rows, heads_dev), jnp.float32),
        jnp.zeros((rows, heads_dev, DH), jnp.float32),
    )


def body(queries, new_keys, new_values, cache_keys, cache_values, positions, cache_len, out_weight):
    tok_dev = queries.shape[0]
    heads_dev = queries.shape[1] // DH
    stripe = cache_keys.shape[0]
    seq_index = lax.axis_index("seq")
    head_index = lax.axis_index(HEAD)
    column = head_index * heads_dev // GQA * DH
    own_keys = jnp.concatenate(
        [
            lax.dynamic_slice_in_dim(cache_keys, column, DH, 1),
            lax.dynamic_slice_in_dim(new_keys, column, DH, 1),
        ],
        axis=0,
    )
    own_values = jnp.concatenate(
        [
            lax.dynamic_slice_in_dim(cache_values, column, DH, 1),
            lax.dynamic_slice_in_dim(new_values, column, DH, 1),
        ],
        axis=0,
    )
    key_block = jnp.concatenate([own_keys, own_values], axis=1)
    query_heads = queries.reshape(tok_dev, heads_dev, DH)
    query_pos = lax.dynamic_slice_in_dim(positions, seq_index * tok_dev, tok_dev)
    stepper = partial(
        softmax_step,
        query_heads=query_heads,
        query_pos=query_pos,
        positions=positions,
        cache_len=cache_len,
        stripe=stripe,
        tok_dev=tok_dev,
    )
    final_max, final_sum, weighted = stepper(
        empty_state(tok_dev, heads_dev),
        lax.all_gather(key_block, "seq", axis=0, tiled=True),
        jnp.int32(0),
    )
    attended = (
        (weighted / final_sum[:, :, None]).astype(jnp.bfloat16).reshape(tok_dev, heads_dev * DH)
    )
    partial_out = jnp.dot(
        gather_directly(attended, "seq", 0), out_weight, preferred_element_type=jnp.float32
    )
    return nested_sum(partial_out, ("head_0", ("head_1", "head_2")))


def solution(mesh):
    torus = Mesh(
        mesh.devices.reshape(mesh.shape["seq"], 2, 4, 4), ("seq", "head_0", "head_1", "head_2")
    )
    return jax.shard_map(
        body,
        mesh=torus,
        in_specs=(
            P("seq", HEAD),
            P("seq", None),
            P("seq", None),
            P("seq", None),
            P("seq", None),
            P(),
            P(),
            P(HEAD, "seq"),
        ),
        out_specs=P(None, "seq"),
        check_vma=False,
    )
```

profile of v0, /device:TPU:1, one launch (start us, length us, event | category | flops | bytes accessed | tf_op | source)
XLA Modules:
  0.0 375.3 jit_solution(1419468475404500871)
XLA Ops:
  6.5 0.0 copy-start
  6.5 0.0 copy-start.1
  6.5 0.0 all-gather.2.cloned.1.call-start
  6.5 0.8 constant_dynamic-slice_fusion.1
  7.4 1.1 constant_dynamic-slice_fusion
  8.4 0.8 maximum_maximum_fusion
  9.2 0.0 all-gather.2.cloned.1.call-update
  9.3 0.8 dynamic_slice.15
  10.0 0.3 compare_select_fusion.1
  10.4 0.0 copy-done.1
  10.4 0.0 copy-start.2
  10.4 0.0 copy-start.3
  10.4 53.1 %gather_fusion = s32[13312]{0:T(1024)S(1)} fusion(s32[1024]{0:T(1024)S(1)} %copy-done.1, s32[13312]{0:T(1024)S(1)} %broadcast_clamp_fusion), kind=kCustom, calls=%fused_computation | custom fusion | bytes 159744 | tf_op jit(solution)/shard_map/jit(_take)/gather | solution.py:79
  63.5 0.0 copy-done.2
  63.5 0.2 select_reduce_fusion
  63.8 0.1 and_select_fusion.2
  63.9 0.7 compare_select_fusion
  64.6 59.7 %all-gather.2.cloned.1.call-done = bf16[13312,256]{1,0:T(8,128)(2,1)} async-done(((bf16[832,256]{1,0:T(8,128)(2,1)}), bf16[13312,256]{1,0:T(8,128)(2,1)}) %all-gather.2.cloned.1.call-update) | async-done | bytes 6815760 | tf_op jit(solution)/shard_map/all_gather | solution.py:148
  124.2 0.0 copy-done.3
  124.2 9.4 %fusion.33 = (f32[64,4]{0,1:T(4,128)S(1)}, f32[64,4,13312]{2,0,1:T(8,128)}) fusion(bf16[13312,256]{1,0:T(8,128)(2,1)} %all-gather.2.cloned.1.call-done, pred[64,13312]{1,0:T(8,128)(4,1)S(1)} %compare_select_fusion, bf16[64,512]{1,0:T(8,128)(2,1)S(1)} %copy-done.3), kind=kOutput, calls=%fused_computation.56 | convolution fusion | flops 882638592 | bytes 17957888 | tf_op jit(solution)/shard_map/thd,kd->thk/dot_general | solution.py:91
  133.6 8.1 %fusion.2 = f32[64,4]{0,1:T(4,128)S(1)} fusion(f32[64,4,13312]{2,0,1:T(8,128)} %get-tuple-element.6, f32[64,4]{0,1:T(4,128)S(1)} %broadcast_maximum_fusion, pred[64,13312]{1,0:T(8,128)(4,1)S(1)} %compare_select_fusion), kind=kLoop, calls=%fused_computation.5 | loop fusion | flops 10223360 | bytes 14485504 | tf_op jit(solution)/shard_map/reduce_sum | solution.py:98
  141.7 8.4 %fusion.15 = bf16[4,8,8,128]{3,2,1,0:T(8,128)(2,1)S(1)} fusion(bf16[13312,256]{1,0:T(8,128)(2,1)} %all-gather.2.cloned.1.call-done, f32[64,4,13312]{2,0,1:T(8,128)} %get-tuple-element.6, f32[64,4]{0,1:T(4,128)S(1)} %broadcast_maximum_fusion, pred[64,13312]{1,0:T(8,128)(4,1)S(1)} %compare_select_fusion, f32[64,4]{0,1:T(4,128)S(1)} %fusion.2), kind=kOutput, calls=%fused_computation.17 | convolution fusion | flops 882704384 | bytes 17958912 | tf_op jit(solution)/shard_map/thk,kd->thd/dot_general | solution.py:99
  150.1 0.1 broadcast_in_dim.83
  150.2 60.3 %all_to_all.25 = bf16[16,64,512]{2,1,0:T(8,128)(2,1)S(1)} all-to-all(bf16[16,64,512]{2,1,0:T(8,128)(2,1)S(1)} %broadcast_in_dim.83), channel_id=1, replica_groups=mesh['seq'=16,'head_0'=2,'head_1'=4,'head_2'=4] {'seq'}, dimensions={0} | all-to-all | bytes 2097152 | tf_op jit(solution)/shard_map/all_to_all | solution.py:16
  210.5 0.0 copy-done
  210.5 1.2 convolution_bitcast_fusion
  211.8 0.6 copy.21
  212.4 55.7 %all_to_all.26 = f32[16,2,32,1024]{3,2,1,0:T(8,128)} all-to-all(f32[16,2,32,1024]{3,2,1,0:T(8,128)S(1)} %copy.21), channel_id=1, replica_groups=mesh['seq'=16,'head_0'=2,'head_1'=4,'head_2'=4] {'head_1','head_2'}, dimensions={0} | all-to-all | bytes 8388608 | tf_op jit(solution)/shard_map/all_to_all | solution.py:38
  268.1 2.5 reduce_sum.38
  270.6 25.3 %all_to_all.27 = f32[2,32,1024]{2,1,0:T(8,128)S(1)} all-to-all(f32[2,32,1024]{2,1,0:T(8,128)S(1)} %reduce_sum.38), channel_id=1, replica_groups=mesh['seq'=16,'head_0'=2,'head_1'=4,'head_2'=4] {'head_0'}, dimensions={0} | all-to-all | bytes 524288 | tf_op jit(solution)/shard_map/all_to_all | solution.py:45
  296.0 15.3 %all_to_all.28 = f32[2,32,1024]{2,1,0:T(8,128)S(1)} all-to-all(f32[2,32,1024]{2,1,0:T(8,128)S(1)} %broadcast_in_dim.84), channel_id=1, replica_groups=mesh['seq'=16,'head_0'=2,'head_1'=4,'head_2'=4] {'head_0'}, dimensions={0} | all-to-all | bytes 524288 | tf_op jit(solution)/shard_map/all_to_all | solution.py:16
  311.2 0.5 broadcast_in_dim.85
  311.8 54.4 %all_to_all.29 = f32[16,2,32,1024]{3,2,1,0:T(8,128)S(1)} all-to-all(f32[16,2,32,1024]{3,2,1,0:T(8,128)S(1)} %broadcast_in_dim.85), channel_id=1, replica_groups=mesh['seq'=16,'head_0'=2,'head_1'=4,'head_2'=4] {'head_1','head_2'}, dimensions={0} | all-to-all | bytes 8388608 | tf_op jit(solution)/shard_map/all_to_all | solution.py:16
  366.2 2.3 copy.22
  (7 shorter events, 0.1 us)
Async XLA Ops:
  6.5 204.0 %copy-start = (bf16[512,1024]{1,0:T(8,128)(2,1)S(1)}, bf16[512,1024]{1,0:T(8,128)(2,1)}, u32[]{:S(2)}) copy-start(bf16[512,1024]{1,0:T(8,128)(2,1)} %param.15) | copy-start | bytes 3145732
  6.5 3.8 %copy-start.1 = (s32[1024]{0:T(1024)S(1)}, s32[1024]{0:T(1024)}, u32[]{:S(2)}) copy-start(s32[1024]{0:T(1024)} %param.13) | copy-start | bytes 12292
  6.5 117.7 %all-gather.2.cloned.1.call-start = ((), (), s32[]{:S(2)}) async-start(), calls=%async_computation.5 | async-start | bytes 7241728 | tf_op jit(solution)/shard_map/all_gather | solution.py:148
  10.4 53.2 %copy-start.2 = (s32[16]{0:T(128)S(1)}, s32[16]{0:T(128)}, u32[]{:S(2)}) copy-start(s32[16]{0:T(128)} %param.14) | copy-start | bytes 196
  10.4 113.8 %copy-start.3 = (bf16[64,512]{1,0:T(8,128)(2,1)S(1)}, bf16[64,512]{1,0:T(8,128)(2,1)}, u32[]{:S(2)}) copy-start(bf16[64,512]{1,0:T(8,128)(2,1)} %param.8) | copy-start | bytes 196612
Sparse Core Ops, SparseCore 0:
  9.4 114.7 all-gather.1
where the time goes:
time: 379 us; the launch traced here: 375 us
  blocking collectives  211 us (56%)
  waiting for transfers between devices  59.7 us (16%)
  local copies, waits for them, and re-layouts  59.3 us (16%)
  matrix products  19 us (5%)
  between operations  13.5 us (4%)
  other arithmetic  12.8 us (3%)
    all_to_all x3, blocking collectives, sent_to_all(): return lax.all_to_all(copies, axis, split_axis=0, concat_axis=0, tiled=True)  130 us
    all_gather x1, waiting for transfers between devices, body(): lax.all_gather(key_block, 'seq', axis=0, tiled=True)  59.7 us
    all_to_all x1, blocking collectives, summed_on_arrival(): blocks = lax.all_to_all(cut_along(x, dim, size), axis, 0, 0, tiled=True)  55.7 us
    gather x1, local copies, waits for them, and re-layouts, key_mask(): key_pos = jnp.take(positions, token)  53.1 us
    all_to_all x1, blocking collectives, sum_in_two_steps(): return jnp.sum(lax.all_to_all(own, far, 0, 0, tiled=True), axis=0)  25.3 us
    dot_general x1, matrix products, softmax_step(): jnp.einsum('thd,kd->thk', query_heads, keys, preferred_element_type=jnp.f...  9.36 us
    dot_general x1, matrix products, softmax_step(): jnp.einsum('thk,kd->thd', expo.astype(jnp.bfloat16), values, preferred_el...  8.36 us
    reduce_sum x1, other arithmetic, softmax_step(): running_sum = jnp.sum(expo, axis=2)  8.14 us
  transfers between devices with their start and end apart: 1, of which 1 were waited for; matrix products, arithmetic and copies ran while one was open for 15% of the time, Pallas kernels for 0%

commit v1 on v0

v1 whole, which is shorter than its diff:
```python
import functools

import jax
import jax.numpy as jnp
from jax import lax
from jax.experimental import pallas as pl
from jax.experimental.pallas import tpu as pltpu
from jax.sharding import Mesh
from jax.sharding import PartitionSpec as P

DH = 128
GQA = 16
LINE = "line"
NEAR = "near"
PAIR = "core"
FAR = "far"
PLANE = ("x", "y")
SEQ = (LINE, NEAR, PAIR)
HEAD = (FAR, *PLANE)
HIDDEN = -1e30
SCALE = DH**-0.5 * 1.4426950408889634
BF16 = jnp.bfloat16
F32 = jnp.float32


def sent_to_all(x, axes):
    copies = jnp.broadcast_to(x, (lax.axis_size(axes), *x.shape))
    return lax.all_to_all(copies, axes, split_axis=0, concat_axis=0, tiled=True)


def attend_kernel(lens_ref, key_pos_ref, query_pos_ref, query_ref, kv_ref, near_kv_ref, out_ref):
    lines, rows, width = query_ref.shape
    heads = width // DH
    tokens = lines * rows
    slices = [ref.at[core] for ref in (kv_ref, near_kv_ref) for core in range(2)]
    stripe = kv_ref.shape[1] - key_pos_ref.shape[1] // len(slices)
    nt = (((1,), (1,)), ((), ()))
    slot = lax.broadcasted_iota(jnp.int32, (1, stripe), 1)
    live = [slot < lens_ref[i] for i in range(len(slices))]
    causal = key_pos_ref[...] <= query_pos_ref[...]
    new_keys = jnp.concatenate([ref[stripe:, :DH] for ref in slices], axis=0)
    new_values = jnp.concatenate([ref[stripe:, DH:] for ref in slices], axis=0)
    lane = lax.broadcasted_iota(jnp.int32, (tokens, DH), 1)
    stats = jnp.zeros((tokens, DH), F32)
    for head in range(heads):
        query = query_ref[:, :, head * DH : (head + 1) * DH].reshape(tokens, DH)
        parts = [
            jnp.where(
                shown,
                lax.dot_general(query, ref[:stripe, :DH], nt, preferred_element_type=F32),
                HIDDEN,
            )
            for shown, ref in zip(live, slices)
        ]
        parts.append(
            jnp.where(
                causal, lax.dot_general(query, new_keys, nt, preferred_element_type=F32), HIDDEN
            )
        )
        peak = functools.reduce(
            jnp.maximum, [jnp.max(part, axis=1, keepdims=True) for part in parts]
        )
        peak = peak.astype(BF16).astype(F32)
        expo = [jnp.exp2((part - peak) * SCALE) for part in parts]
        total = sum(jnp.sum(part, axis=1, keepdims=True) for part in expo)
        values = [ref[:stripe, DH:] for ref in slices] + [new_values]
        mixed = sum(
            jnp.dot(part.astype(BF16), value, preferred_element_type=F32)
            for part, value in zip(expo, values)
        )
        out_ref[:, :, head * DH : (head + 1) * DH] = mixed.astype(BF16).reshape(lines, rows, DH)
        coarse = total.astype(BF16).astype(F32)
        stats = jnp.where(lane == head, peak, stats)
        stats = jnp.where(lane == heads + head, coarse, stats)
        stats = jnp.where(lane == 2 * heads + head, total - coarse, stats)
    out_ref[:, :, width:] = stats.astype(BF16).reshape(lines, rows, DH)


def attend(lens, key_pos, query_pos, queries, kv, near_kv):
    lines, rows, width = queries.shape
    work = lines * rows * (width // DH) * 4 * kv.shape[1]
    vmem = pl.BlockSpec(memory_space=pltpu.VMEM)
    return pl.pallas_call(
        attend_kernel,
        out_shape=jax.ShapeDtypeStruct((lines, rows, width + DH), BF16),
        in_specs=[pl.BlockSpec(memory_space=pltpu.SMEM), vmem, vmem, vmem, vmem, vmem],
        out_specs=vmem,
        compiler_params=pltpu.CompilerParams(vmem_limit_bytes=40 << 20),
        cost_estimate=pl.CostEstimate(
            flops=4 * work * DH, transcendentals=work, bytes_accessed=4 * (queries.size + kv.size)
        ),
        name="attend",
    )(lens, key_pos, query_pos, queries, kv, near_kv)


def combine_kernel(part_ref, out_ref):
    width = out_ref.shape[1]
    heads = width // DH
    stats = part_ref[:, :, width:].astype(F32)
    for head in range(heads):
        peaks = stats[:, :, head : head + 1]
        sums = (
            stats[:, :, heads + head : heads + head + 1]
            + stats[:, :, 2 * heads + head : 2 * heads + head + 1]
        )
        scale = jnp.exp2((peaks - jnp.max(peaks, axis=0, keepdims=True)) * SCALE)
        scale = scale / jnp.sum(scale * sums, axis=0, keepdims=True)
        columns = slice(head * DH, (head + 1) * DH)
        mixed = jnp.sum(part_ref[:, :, columns].astype(F32) * scale, axis=0)
        out_ref[:, columns] = mixed.astype(BF16)


def combine(parts):
    lines, rows, width = parts.shape
    vmem = pl.BlockSpec(memory_space=pltpu.VMEM)
    return pl.pallas_call(
        combine_kernel,
        out_shape=jax.ShapeDtypeStruct((rows, width - DH), BF16),
        in_specs=[vmem],
        out_specs=vmem,
        cost_estimate=pl.CostEstimate(
            flops=2 * parts.size, transcendentals=0, bytes_accessed=2 * parts.size
        ),
        name="combine",
    )(parts)


def body(queries, new_keys, new_values, cache_keys, cache_values, positions, cache_len, out_weight):
    tok_dev, width = queries.shape
    heads_dev = width // DH
    lines, near, pair = (lax.axis_size(axis) for axis in SEQ)
    line, side, core = (lax.axis_index(axis) for axis in SEQ)
    column = lax.axis_index(HEAD) * heads_dev // GQA * DH

    def own(x):
        return lax.dynamic_slice_in_dim(x, column, DH, 1)

    kv = jnp.concatenate(
        [
            jnp.concatenate([own(cache_keys), own(new_keys)], axis=0),
            jnp.concatenate([own(cache_values), own(new_values)], axis=0),
        ],
        axis=1,
    )
    near_kv = lax.all_gather(lax.ppermute(kv, NEAR, [(0, 1), (1, 0)]), PAIR)
    kv = lax.all_gather(kv, PAIR)
    chips = [line * near + side, line * near + 1 - side]
    lens = jnp.concatenate(
        [lax.dynamic_slice_in_dim(cache_len, chip * pair, pair) for chip in chips]
    )
    key_pos = jnp.concatenate(
        [
            lax.dynamic_slice_in_dim(positions, chip * pair * tok_dev, pair * tok_dev)
            for chip in chips
        ]
    )[None, :]
    query_pos = lax.dynamic_index_in_dim(
        positions.reshape(lines, near * pair, tok_dev), side * pair + core, 1, keepdims=False
    ).reshape(lines * tok_dev, 1)

    partial_rows = attend(lens, key_pos, query_pos, sent_to_all(queries, LINE), kv, near_kv)
    attended = combine(lax.all_to_all(partial_rows, LINE, 0, 0, tiled=True))
    attended = sent_to_all(attended, (LINE, NEAR))
    other = lax.ppermute(attended, PAIR, [(0, 1), (1, 0)])
    first = core == 0
    attended = jnp.stack(
        [jnp.where(first, attended, other), jnp.where(first, other, attended)], axis=1
    )
    partial_out = jnp.dot(
        attended.reshape(-1, width), out_weight, preferred_element_type=F32
    ).astype(BF16)
    blocks = partial_out.reshape(lines * near * pair, tok_dev, -1)
    arrived = lax.all_to_all(blocks, PLANE, 0, 0, tiled=True)
    summed = jnp.sum(arrived.astype(F32), axis=0).astype(BF16)
    far = lax.ppermute(summed, FAR, [(0, 1), (1, 0)])
    whole = (summed.astype(F32) + far.astype(F32)).astype(BF16)
    return sent_to_all(whole, PLANE).reshape(partial_out.shape).astype(F32)


def solution(mesh):
    torus = Mesh(mesh.devices.reshape(4, 2, 2, 2, 4, 4), (*SEQ, *HEAD))
    return jax.shard_map(
        body,
        mesh=torus,
        in_specs=(
            P(SEQ, HEAD),
            P(SEQ, None),
            P(SEQ, None),
            P(SEQ, None),
            P(SEQ, None),
            P(),
            P(),
            P(HEAD, SEQ),
        ),
        out_specs=P(None, SEQ),
        check_vma=False,
    )
```

time: 379 us -> 204 us (0.54)
  blocking collectives: 211 us -> 129 us
  local copies, waits for them, and re-layouts: 59.3 us -> 4.98 us
  waiting for transfers between devices: 59.7 us -> 24.4 us
  starting transfers between devices: 0.01 us -> 32.8 us
  matrix products: 19 us -> 1.26 us
  between operations: 13.5 us -> 0.14 us
  other arithmetic: 12.8 us -> 3.35 us
  Pallas kernels: 0 us -> 7.85 us
    all_to_all x5 -> x4, blocking collectives: 211 us -> 122 us  [the longest x2 57.9 us: sent_to_all(): return lax.all_to_all(copies, axes, split_axis=0, concat_axis=0, tiled=True)]
    all_gather x1 -> x0, waiting for transfers between devices: 59.7 us -> none  [body(): lax.all_gather(key_block, 'seq', axis=0, tiled=True)]
    gather x1 -> x0, local copies, waits for them, and re-layouts: 53.1 us -> none  [key_mask(): key_pos = jnp.take(positions, token)]
    ppermute x0 -> x3, waiting for transfers between devices: none -> 24.3 us  [the longest x1 14.5 us: body(): far = lax.ppermute(summed, FAR, [(0, 1), (1, 0)])]
    ppermute x0 -> x3, starting transfers between devices: none -> 21.1 us  [the longest x1 8.87 us: body(): other = lax.ppermute(attended, PAIR, [(0, 1), (1, 0)])]
    dot_general x3 -> x1, matrix products: 19 us -> 1.26 us  [body(): jnp.dot(attended.reshape(-1, width), out_weight, preferred_element_type=F32)]
    all_to_all x0 -> x1, starting transfers between devices: none -> 11.7 us  [sent_to_all(): return lax.all_to_all(copies, axes, split_axis=0, concat_axis=0, tiled=True)]
    reduce_sum x4 -> x1, other arithmetic: 10.9 us -> 0.4 us  [body(): summed = jnp.sum(arrived.astype(F32), axis=0).astype(BF16)]
  transfers between devices with their start and end apart: 1 -> 4, of which waited for: 1 -> 3; matrix products, arithmetic and copies ran while one was open for 15% -> 1% of each run, Pallas kernels for 0% -> 0%
where the time goes in v1:
time: 204 us
  blocking collectives  129 us (63%)
  starting transfers between devices  32.8 us (16%)
  waiting for transfers between devices  24.4 us (12%)
  Pallas kernels  7.85 us (4%)
  local copies, waits for them, and re-layouts  4.98 us (2%)
  other arithmetic  3.35 us (2%)
    all_to_all x2, blocking collectives, sent_to_all(): return lax.all_to_all(copies, axes, split_axis=0, concat_axis=0, tiled=True)  57.9 us
    all_to_all x1, blocking collectives, body(): arrived = lax.all_to_all(blocks, PLANE, 0, 0, tiled=True)  33.8 us
    all_to_all x1, blocking collectives, body(): attended = combine(lax.all_to_all(partial_rows, LINE, 0, 0, tiled=True))  30.3 us
    ppermute x1, waiting for transfers between devices, body(): far = lax.ppermute(summed, FAR, [(0, 1), (1, 0)])  14.5 us
    all_to_all x1, starting transfers between devices, sent_to_all(): return lax.all_to_all(copies, axes, split_axis=0, concat_axis=0, tiled=True)  11.7 us
    ppermute x1, starting transfers between devices, body(): other = lax.ppermute(attended, PAIR, [(0, 1), (1, 0)])  8.87 us
    ppermute x1, starting transfers between devices, body(): far = lax.ppermute(summed, FAR, [(0, 1), (1, 0)])  8.68 us
    ppermute x1, waiting for transfers between devices, body(): near_kv = lax.all_gather(lax.ppermute(kv, NEAR, [(0, 1), (1, 0)]), PAIR)  8.34 us
  transfers between devices with their start and end apart: 4, of which 3 were waited for; matrix products, arithmetic and copies ran while one was open for 1% of the time, Pallas kernels for 0%

profile of v1, /device:TPU:1, one launch (start us, length us, event | category | flops | bytes accessed | tf_op | source)
XLA Modules:
  0.0 203.8 jit_solution(9313947955862739527)
XLA Ops:
  0.0 0.0 copy-start
  0.0 0.0 copy-start.1
  0.0 0.0 copy-start.2
  0.0 1.6 broadcast_in_dim.13
  1.7 11.7 %all-to-all-start = ((bf16[4,64,512]{2,1,0:T(8,128)(2,1)}), bf16[4,64,512]{2,1,0:T(8,128)(2,1)S(1)}, u32[]{:S(2)}, u32[]{:S(2)}) async-start(bf16[4,64,512]{2,1,0:T(8,128)(2,1)} %broadcast_in_dim.13), calls=%async_computation | async-start | bytes 524288 | tf_op jit(solution)/shard_map/all_to_all | solution.py:28
  13.4 0.7 constant_dynamic-slice_fusion
  14.1 1.1 constant_dynamic-slice_fusion.1
  15.2 3.5 %collective-permute-start = (bf16[832,256]{1,0:T(8,128)(2,1)S(1)}, bf16[832,256]{1,0:T(8,128)(2,1)}, u32[]{:S(2)}, u32[]{:S(2)}) collective-permute-start(bf16[832,256]{1,0:T(8,128)(2,1)S(1)} %maximum_maximum_fusion), channel_id=1, source_target_pairs={{0,64},{64,0},{1,65},{65,1},{2,66},{66,2},{3,67},{67,3},{4,68},{68... | collective-permute-start | bytes 1277960 | tf_op jit(solution)/shard_map/ppermute | solution.py:145
  18.8 0.0 copy-done.1
  18.8 0.1 fusion
  18.9 0.1 reshape.16
  19.0 0.1 reshape.23.query_pos_ref
  19.1 0.0 copy-done.2
  19.1 0.1 fusion.1
  19.2 0.1 pad_add_fusion.1.lens_ref
  19.3 3.3 %all-gather = bf16[1664,256]{1,0:T(8,128)(2,1)S(1)} all-gather(bf16[832,256]{1,0:T(8,128)(2,1)S(1)} %maximum_maximum_fusion), channel_id=2, replica_groups=mesh['line'=4,'near'=2,'core'=2,'far'=2,'x'=4,'y'=4] {'core'}, dimensions={0}, use_global_device_ids=true | all-gather | bytes 1277952 | tf_op jit(solution)/shard_map/all_gather | solution.py:146
  22.6 8.3 %collective-permute-done = bf16[832,256]{1,0:T(8,128)(2,1)} collective-permute-done((bf16[832,256]{1,0:T(8,128)(2,1)S(1)}, bf16[832,256]{1,0:T(8,128)(2,1)}, u32[]{:S(2)}, u32[]{:S(2)}) %collective-permute-start) | collective-permute-done | bytes 426016 | tf_op jit(solution)/shard_map/ppermute | solution.py:145
  30.9 3.8 %all-gather.1 = bf16[1664,256]{1,0:T(8,128)(2,1)S(1)} all-gather(bf16[832,256]{1,0:T(8,128)(2,1)} %collective-permute-done), channel_id=3, replica_groups=mesh['line'=4,'near'=2,'core'=2,'far'=2,'x'=4,'y'=4] {'core'}, dimensions={0}, use_global_device_ids=true | all-gather | bytes 1277952 | tf_op jit(solution)/shard_map/all_gather | solution.py:145
  34.7 0.0 all-to-all-done.query_ref
  34.7 5.8 %attend.1 = bf16[4,64,640]{2,1,0:T(8,128)(2,1)S(1)} custom-call(s32[4]{0:T(128)S(1)} %pad_add_fusion.1.lens_ref, s32[1,256]{1,0:T(1,128)S(1)} %bitcast.18, s32[256,1]{1,0:T(8,128)S(1)} %reshape.23.query_pos_ref, bf16[4,64,512]{2,1,0:T(8,128)(2,1)S(1)} %all-to-all-done.query_ref, bf16[2,832,256]{2,1,0:T(8,128)(2,1)S(1)} %bitcast.16, ...), custom_call_target="tpu_custom_call" | custom-call | flops 1744830464 | bytes 2228224 | tf_op jit(solution)/shard_map/attend/pallas_call | solution.py:83
  40.5 30.3 %all_to_all.25.part_ref = bf16[4,64,640]{2,1,0:T(8,128)(2,1)} all-to-all(bf16[4,64,640]{2,1,0:T(8,128)(2,1)S(1)} %attend.1), channel_id=1, replica_groups=mesh['line'=4,'near'=2,'core'=2,'far'=2,'x'=4,'y'=4] {'line'}, dimensions={0} | all-to-all | bytes 655360 | tf_op jit(solution)/shard_map/all_to_all | solution.py:162
  70.9 2.0 combine.1
  72.9 0.9 broadcast_in_dim.14
  73.8 26.4 %all_to_all.26 = bf16[8,64,512]{2,1,0:T(8,128)(2,1)S(1)} all-to-all(bf16[8,64,512]{2,1,0:T(8,128)(2,1)S(1)} %broadcast_in_dim.14), channel_id=1, replica_groups=mesh['line'=4,'near'=2,'core'=2,'far'=2,'x'=4,'y'=4] {'line','near'}, dimensions={0} | all-to-all | bytes 1048576 | tf_op jit(solution)/shard_map/all_to_all | solution.py:28
  100.2 8.9 %collective-permute-start.1 = (bf16[8,64,512]{2,1,0:T(8,128)(2,1)S(1)}, bf16[8,64,512]{2,1,0:T(8,128)(2,1)S(1)}, u32[]{:S(2)}, u32[]{:S(2)}) collective-permute-start(bf16[8,64,512]{2,1,0:T(8,128)(2,1)S(1)} %all_to_all.26), channel_id=1, source_target_pairs={{0,32},{32,0},{1,33},{33,1},{2,34},{34,2},{3,35},{35,3},{4,36},{36... | collective-permute-start | bytes 1572872 | tf_op jit(solution)/shard_map/ppermute | solution.py:164
  109.1 1.5 collective-permute-done.1
  110.6 0.1 select_bitcast_fusion.1
  110.7 0.1 pad_maximum_fusion
  110.8 0.0 copy-done
  110.8 1.3 convolution_convert_fusion
  112.1 33.8 %all_to_all.27 = bf16[16,64,1024]{2,1,0:T(8,128)(2,1)S(1)} all-to-all(bf16[16,64,1024]{2,1,0:T(8,128)(2,1)S(1)} %bitcast.19), channel_id=1, replica_groups=mesh['line'=4,'near'=2,'core'=2,'far'=2,'x'=4,'y'=4] {'x','y'}, dimensions={0} | all-to-all | bytes 4194304 | tf_op jit(solution)/shard_map/all_to_all | solution.py:173
  145.8 0.4 reduce_sum.12
  146.2 8.7 %collective-permute-start.2 = (bf16[64,1024]{1,0:T(8,128)(2,1)S(1)}, bf16[64,1024]{1,0:T(8,128)(2,1)S(1)}, u32[]{:S(2)}, u32[]{:S(2)}) collective-permute-start(bf16[64,1024]{1,0:T(8,128)(2,1)S(1)} %reduce_sum.12), channel_id=1, source_target_pairs={{0,16},{16,0},{1,17},{17,1},{2,18},{18,2},{3,19},{19,3},{4,20},{20... | collective-permute-start | bytes 393224 | tf_op jit(solution)/shard_map/ppermute | solution.py:175
  154.9 14.5 %collective-permute-done.2 = bf16[64,1024]{1,0:T(8,128)(2,1)S(1)} collective-permute-done((bf16[64,1024]{1,0:T(8,128)(2,1)S(1)}, bf16[64,1024]{1,0:T(8,128)(2,1)S(1)}, u32[]{:S(2)}, u32[]{:S(2)}) %collective-permute-start.2) | collective-permute-done | bytes 131104 | tf_op jit(solution)/shard_map/ppermute | solution.py:175
  169.5 0.3 broadcast_in_dim.15
  169.7 31.4 %all_to_all.28 = bf16[16,64,1024]{2,1,0:T(8,128)(2,1)S(1)} all-to-all(bf16[16,64,1024]{2,1,0:T(8,128)(2,1)S(1)} %broadcast_in_dim.15), channel_id=1, replica_groups=mesh['line'=4,'near'=2,'core'=2,'far'=2,'x'=4,'y'=4] {'x','y'}, dimensions={0} | all-to-all | bytes 4194304 | tf_op jit(solution)/shard_map/all_to_all | solution.py:28
  201.1 2.6 %bitcast_convert_fusion = f32[1024,1024]{1,0:T(8,128)} fusion(bf16[16,64,1024]{2,1,0:T(8,128)(2,1)S(1)} %all_to_all.28), kind=kLoop, calls=%fused_computation | loop fusion | flops 1048576 | bytes 6291456 | tf_op jit(solution)/shard_map/convert_element_type | solution.py:177
  (4 shorter events, 0.1 us)
Async XLA Ops:
  0.0 110.8 %copy-start = (bf16[512,1024]{1,0:T(8,128)(2,1)S(1)}, bf16[512,1024]{1,0:T(8,128)(2,1)}, u32[]{:S(2)}) copy-start(bf16[512,1024]{1,0:T(8,128)(2,1)} %param.15) | copy-start | bytes 3145732
  0.0 18.8 %copy-start.1 = (s32[1024]{0:T(1024)S(1)}, s32[1024]{0:T(1024)}, u32[]{:S(2)}) copy-start(s32[1024]{0:T(1024)} %param.13) | copy-start | bytes 12292
  0.0 19.1 %copy-start.2 = (s32[16]{0:T(128)S(1)}, s32[16]{0:T(128)}, u32[]{:S(2)}) copy-start(s32[16]{0:T(128)} %param.14) | copy-start | bytes 196
  1.7 33.0 %all-to-all-start = ((bf16[4,64,512]{2,1,0:T(8,128)(2,1)}), bf16[4,64,512]{2,1,0:T(8,128)(2,1)S(1)}, u32[]{:S(2)}, u32[]{:S(2)}) async-start(bf16[4,64,512]{2,1,0:T(8,128)(2,1)} %broadcast_in_dim.13), calls=%async_computation | async-start | bytes 524288 | tf_op jit(solution)/shard_map/all_to_all | solution.py:28
  15.2 15.7 %collective-permute-start = (bf16[832,256]{1,0:T(8,128)(2,1)S(1)}, bf16[832,256]{1,0:T(8,128)(2,1)}, u32[]{:S(2)}, u32[]{:S(2)}) collective-permute-start(bf16[832,256]{1,0:T(8,128)(2,1)S(1)} %maximum_maximum_fusion), channel_id=1, source_target_pairs={{0,64},{64,0},{1,65},{65,1},{2,66},{66,2},{3,67},{67,3},{4,68},{68... | collective-permute-start | bytes 1277960 | tf_op jit(solution)/shard_map/ppermute | solution.py:145
  100.2 10.4 %collective-permute-start.1 = (bf16[8,64,512]{2,1,0:T(8,128)(2,1)S(1)}, bf16[8,64,512]{2,1,0:T(8,128)(2,1)S(1)}, u32[]{:S(2)}, u32[]{:S(2)}) collective-permute-start(bf16[8,64,512]{2,1,0:T(8,128)(2,1)S(1)} %all_to_all.26), channel_id=1, source_target_pairs={{0,32},{32,0},{1,33},{33,1},{2,34},{34,2},{3,35},{35,3},{4,36},{36... | collective-permute-start | bytes 1572872 | tf_op jit(solution)/shard_map/ppermute | solution.py:164
  146.2 23.2 %collective-permute-start.2 = (bf16[64,1024]{1,0:T(8,128)(2,1)S(1)}, bf16[64,1024]{1,0:T(8,128)(2,1)S(1)}, u32[]{:S(2)}, u32[]{:S(2)}) collective-permute-start(bf16[64,1024]{1,0:T(8,128)(2,1)S(1)} %reduce_sum.12), channel_id=1, source_target_pairs={{0,16},{16,0},{1,17},{17,1},{2,18},{18,2},{3,19},{19,3},{4,20},{20... | collective-permute-start | bytes 393224 | tf_op jit(solution)/shard_map/ppermute | solution.py:175

commit v2 on v1

--- a/solution.py
+++ b/solution.py
@@ -118,11 +118,48 @@
         out_shape=jax.ShapeDtypeStruct((rows, width - DH), BF16),
         in_specs=[vmem],
         out_specs=vmem,
+        compiler_params=pltpu.CompilerParams(vmem_limit_bytes=8 << 20),
         cost_estimate=pl.CostEstimate(
             flops=2 * parts.size, transcendentals=0, bytes_accessed=2 * parts.size
         ),
         name="combine",
     )(parts)
+
+
+def swapped(x, axis, mask=1):
+    return lax.ppermute(x, axis, [(i, i ^ mask) for i in range(lax.axis_size(axis))])
+
+
+def after(x, *others):
+    return lax.optimization_barrier((x, *others))[0]
+
+
+def plane_groups():
+    along_x = [[x * 4 + y for x in range(4)] for y in range(4)]
+    along_y = [[x * 4 + y for y in range(4)] for x in range(4)]
+
+    def both(even, odd):
+        return even + [[16 + index for index in group] for group in odd]
+
+    return both(along_x, along_y), both(along_y, along_x)
+
+
+def exchanged(blocks, groups):
+    return lax.all_to_all(blocks, (PAIR, *PLANE), 0, 0, axis_index_groups=groups, tiled=True)
+
+
+def summed_on_arrival(blocks, groups):
+    return jnp.sum(exchanged(blocks, groups).astype(F32), axis=0).astype(BF16)
+
+
+def sent_within(x, groups):
+    return exchanged(jnp.broadcast_to(x, (len(groups[0]), *x.shape)), groups)
+
+
+def joined(x, axis, dim):
+    other = swapped(x, axis)
+    first = lax.axis_index(axis) == 0
+    return jnp.stack([jnp.where(first, x, other), jnp.where(first, other, x)], axis=dim)
 
 
 def body(queries, new_keys, new_values, cache_keys, cache_values, positions, cache_len, out_weight):
@@ -135,15 +172,15 @@
     def own(x):
         return lax.dynamic_slice_in_dim(x, column, DH, 1)
 
-    kv = jnp.concatenate(
+    own_kv = jnp.concatenate(
         [
             jnp.concatenate([own(cache_keys), own(new_keys)], axis=0),
             jnp.concatenate([own(cache_values), own(new_values)], axis=0),
         ],
         axis=1,
     )
-    near_kv = lax.all_gather(lax.ppermute(kv, NEAR, [(0, 1), (1, 0)]), PAIR)
-    kv = lax.all_gather(kv, PAIR)
+    near_kv = lax.all_gather(swapped(own_kv, NEAR), PAIR)
+    kv = lax.all_gather(own_kv, PAIR)
     chips = [line * near + side, line * near + 1 - side]
     lens = jnp.concatenate(
         [lax.dynamic_slice_in_dim(cache_len, chip * pair, pair) for chip in chips]
@@ -157,24 +194,18 @@
     query_pos = lax.dynamic_index_in_dim(
         positions.reshape(lines, near * pair, tok_dev), side * pair + core, 1, keepdims=False
     ).reshape(lines * tok_dev, 1)
-
-    partial_rows = attend(lens, key_pos, query_pos, sent_to_all(queries, LINE), kv, near_kv)
+    everyone = sent_to_all(after(queries, own_kv), LINE)
+
+    partial_rows = attend(lens, key_pos, query_pos, everyone, kv, near_kv)
     attended = combine(lax.all_to_all(partial_rows, LINE, 0, 0, tiled=True))
-    attended = sent_to_all(attended, (LINE, NEAR))
-    other = lax.ppermute(attended, PAIR, [(0, 1), (1, 0)])
-    first = core == 0
-    attended = jnp.stack(
-        [jnp.where(first, attended, other), jnp.where(first, other, attended)], axis=1
-    )
-    partial_out = jnp.dot(
-        attended.reshape(-1, width), out_weight, preferred_element_type=F32
-    ).astype(BF16)
-    blocks = partial_out.reshape(lines * near * pair, tok_dev, -1)
-    arrived = lax.all_to_all(blocks, PLANE, 0, 0, tiled=True)
-    summed = jnp.sum(arrived.astype(F32), axis=0).astype(BF16)
-    far = lax.ppermute(summed, FAR, [(0, 1), (1, 0)])
-    whole = (summed.astype(F32) + far.astype(F32)).astype(BF16)
-    return sent_to_all(whole, PLANE).reshape(partial_out.shape).astype(F32)
+    attended = joined(sent_to_all(attended, (LINE, NEAR)), PAIR, 1).reshape(-1, width)
+    partial_out = jnp.dot(attended, out_weight, preferred_element_type=F32).astype(BF16)
+    first, second = plane_groups()
+    blocks = partial_out.reshape(4, 4, tok_dev, -1)
+    blocks = summed_on_arrival(summed_on_arrival(blocks, first), second)
+    whole = (blocks.astype(F32) + swapped(blocks, FAR).astype(F32)).astype(BF16)
+    whole = sent_within(sent_within(whole, second), first)
+    return whole.reshape(partial_out.shape).astype(F32)
 
 
 def solution(mesh):

time: 204 us -> 188 us (0.922)
  blocking collectives: 129 us -> 113 us
  starting transfers between devices: 32.8 us -> 30.3 us
    all_to_all x2 -> x1, blocking collectives: 57.9 us -> 26 us  [sent_to_all(): return lax.all_to_all(copies, axes, split_axis=0, concat_axis=0, tiled=True)]
    all_to_all x1 -> x4, blocking collectives: 33.8 us -> 58 us  [exchanged(): lax.all_to_all(blocks, (PAIR, *PLANE), 0, 0, axis_index_groups=groups, ti...]
    all_to_all x1, waiting for transfers between devices: 0.01 us -> 11.3 us  [sent_to_all(): return lax.all_to_all(copies, axes, split_axis=0, concat_axis=0, tiled=True)]
    ppermute x3, waiting for transfers between devices: 24.3 us -> 15 us  [swapped(): lax.ppermute(x, axis, [(i, i ^ mask) for i in range(lax.axis_size(axis))])]
    all_to_all x1, blocking collectives: 30.3 us -> 22.8 us  [body(): attended = combine(lax.all_to_all(partial_rows, LINE, 0, 0, tiled=True))]
where the time goes in v2:
time: 188 us; the launch traced here: 186 us
  blocking collectives  113 us (60%)
  starting transfers between devices  30.3 us (16%)
  waiting for transfers between devices  26.3 us (14%)
  Pallas kernels  6.52 us (3%)
  other arithmetic  4.35 us (2%)
  local copies, waits for them, and re-layouts  4.19 us (2%)
    all_to_all x4, blocking collectives, exchanged(): lax.all_to_all(blocks, (PAIR, *PLANE), 0, 0, axis_index_groups=groups, ti...  58 us
    all_to_all x1, blocking collectives, sent_to_all(): return lax.all_to_all(copies, axes, split_axis=0, concat_axis=0, tiled=True)  26 us
    all_to_all x1, blocking collectives, body(): attended = combine(lax.all_to_all(partial_rows, LINE, 0, 0, tiled=True))  22.8 us
    ppermute x3, starting transfers between devices, swapped(): lax.ppermute(x, axis, [(i, i ^ mask) for i in range(lax.axis_size(axis))])  19.4 us
    ppermute x3, waiting for transfers between devices, swapped(): lax.ppermute(x, axis, [(i, i ^ mask) for i in range(lax.axis_size(axis))])  15 us
    all_to_all x1, waiting for transfers between devices, sent_to_all(): return lax.all_to_all(copies, axes, split_axis=0, concat_axis=0, tiled=True)  11.3 us
    all_to_all x1, starting transfers between devices, sent_to_all(): return lax.all_to_all(copies, axes, split_axis=0, concat_axis=0, tiled=True)  10.9 us
    pallas_call x1, Pallas kernels, attend(): pl.pallas_call(attend_kernel, out_shape=jax.ShapeDtypeStruct((lines, rows...  6.12 us
  transfers between devices with their start and end apart: 4, of which 3 were waited for; matrix products, arithmetic and copies ran while one was open for 1% of the time, Pallas kernels for 0%

profile of v2, /device:TPU:1, one launch (start us, length us, event | category | flops | bytes accessed | tf_op | source)
XLA Modules:
  0.0 185.9 jit_solution(16315585147139937499)
XLA Ops:
  0.0 0.0 copy-start
  0.0 0.0 copy-start.1
  0.0 0.0 copy-start.2
  0.0 0.8 constant_dynamic-slice_fusion
  0.9 1.1 constant_dynamic-slice_fusion.1
  2.0 4.4 %collective-permute-start = (bf16[832,256]{1,0:T(8,128)(2,1)S(1)}, bf16[832,256]{1,0:T(8,128)(2,1)}, u32[]{:S(2)}, u32[]{:S(2)}) collective-permute-start(bf16[832,256]{1,0:T(8,128)(2,1)S(1)} %maximum_maximum_fusion), channel_id=1, source_target_pairs={{0,64},{64,0},{1,65},{65,1},{2,66},{66,2},{3,67},{67,3},{4,68},{68... | collective-permute-start | bytes 1277960 | tf_op jit(solution)/shard_map/ppermute | solution.py:130
  6.4 1.6 broadcast_in_dim.16
  7.9 10.9 %all-to-all-start = ((bf16[4,64,512]{2,1,0:T(8,128)(2,1)}), bf16[4,64,512]{2,1,0:T(8,128)(2,1)S(1)}, u32[]{:S(2)}, u32[]{:S(2)}) async-start(bf16[4,64,512]{2,1,0:T(8,128)(2,1)} %broadcast_in_dim.16), calls=%async_computation | async-start | bytes 524288 | tf_op jit(solution)/shard_map/all_to_all | solution.py:28
  18.8 0.0 copy-done.1
  18.8 0.1 fusion
  18.9 0.1 reshape.16
  19.0 0.1 reshape.23.query_pos_ref
  19.1 0.0 copy-done.2
  19.1 0.1 fusion.1
  19.2 0.1 pad_add_fusion.1.lens_ref
  19.3 3.3 %all-gather = bf16[1664,256]{1,0:T(8,128)(2,1)S(1)} all-gather(bf16[832,256]{1,0:T(8,128)(2,1)S(1)} %maximum_maximum_fusion), channel_id=2, replica_groups=mesh['line'=4,'near'=2,'core'=2,'far'=2,'x'=4,'y'=4] {'core'}, dimensions={0}, use_global_device_ids=true | all-gather | bytes 1277952 | tf_op jit(solution)/shard_map/all_gather | solution.py:183
  22.6 0.0 collective-permute-done
  22.6 2.6 %all-gather.1 = bf16[1664,256]{1,0:T(8,128)(2,1)S(1)} all-gather(bf16[832,256]{1,0:T(8,128)(2,1)} %collective-permute-done), channel_id=3, replica_groups=mesh['line'=4,'near'=2,'core'=2,'far'=2,'x'=4,'y'=4] {'core'}, dimensions={0}, use_global_device_ids=true | all-gather | bytes 1277952 | tf_op jit(solution)/shard_map/all_gather | solution.py:182
  25.2 11.3 %all-to-all-done.query_ref = bf16[4,64,512]{2,1,0:T(8,128)(2,1)S(1)} async-done(((bf16[4,64,512]{2,1,0:T(8,128)(2,1)}), bf16[4,64,512]{2,1,0:T(8,128)(2,1)S(1)}, u32[]{:S(2)}, u32[]{:S(2)}) %all-to-all-start) | async-done | bytes 262176 | tf_op jit(solution)/shard_map/all_to_all | solution.py:28
  36.5 6.1 %attend.1 = bf16[4,64,640]{2,1,0:T(8,128)(2,1)S(1)} custom-call(s32[4]{0:T(128)S(1)} %pad_add_fusion.1.lens_ref, s32[1,256]{1,0:T(1,128)S(1)} %bitcast.18, s32[256,1]{1,0:T(8,128)S(1)} %reshape.23.query_pos_ref, bf16[4,64,512]{2,1,0:T(8,128)(2,1)S(1)} %all-to-all-done.query_ref, bf16[2,832,256]{2,1,0:T(8,128)(2,1)S(1)} %bitcast.16, ...), custom_call_target="tpu_custom_call" | custom-call | flops 1744830464 | bytes 2228224 | tf_op jit(solution)/shard_map/attend/pallas_call | solution.py:83
  42.6 22.8 %all_to_all.35.part_ref = bf16[4,64,640]{2,1,0:T(8,128)(2,1)S(1)} all-to-all(bf16[4,64,640]{2,1,0:T(8,128)(2,1)S(1)} %attend.1), channel_id=1, replica_groups=mesh['line'=4,'near'=2,'core'=2,'far'=2,'x'=4,'y'=4] {'line'}, dimensions={0} | all-to-all | bytes 655360 | tf_op jit(solution)/shard_map/all_to_all | solution.py:200
  65.5 0.4 combine.1
  65.9 26.0 %all_to_all.36 = bf16[8,64,512]{2,1,0:T(8,128)(2,1)S(1)} all-to-all(bf16[8,64,512]{2,1,0:T(8,128)(2,1)S(1)} %broadcast_in_dim.17), channel_id=1, replica_groups=mesh['line'=4,'near'=2,'core'=2,'far'=2,'x'=4,'y'=4] {'line','near'}, dimensions={0} | all-to-all | bytes 1048576 | tf_op jit(solution)/shard_map/all_to_all | solution.py:28
  91.9 8.9 %collective-permute-start.1 = (bf16[8,64,512]{2,1,0:T(8,128)(2,1)S(1)}, bf16[8,64,512]{2,1,0:T(8,128)(2,1)S(1)}, u32[]{:S(2)}, u32[]{:S(2)}) collective-permute-start(bf16[8,64,512]{2,1,0:T(8,128)(2,1)S(1)} %all_to_all.36), channel_id=1, source_target_pairs={{0,32},{32,0},{1,33},{33,1},{2,34},{34,2},{3,35},{35,3},{4,36},{36... | collective-permute-start | bytes 1572872 | tf_op jit(solution)/shard_map/ppermute | solution.py:130
  100.8 1.5 collective-permute-done.1
  102.3 0.1 select_bitcast_fusion.1
  102.4 0.1 pad_maximum_fusion
  102.5 0.0 copy-done
  102.5 1.3 convolution_convert_fusion
  103.8 19.6 %all_to_all.37 = bf16[4,4,64,1024]{3,2,1,0:T(8,128)(2,1)S(1)} all-to-all(bf16[4,4,64,1024]{3,2,1,0:T(8,128)(2,1)S(1)} %bitcast.19), channel_id=1, replica_groups={{0,4,8,12},{1,5,9,13},{2,6,10,14},{3,7,11,15},{32,33,34,35},{36,37,38,3..., dimensions={0} | all-to-all | bytes 4194304 | tf_op jit(solution)/shard_map/all_to_all | solution.py:148
  123.4 1.3 reduce_sum.24
  124.7 10.6 %all_to_all.38 = bf16[4,64,1024]{2,1,0:T(8,128)(2,1)S(1)} all-to-all(bf16[4,64,1024]{2,1,0:T(8,128)(2,1)} %reduce_sum.24), channel_id=1, replica_groups={{0,1,2,3},{4,5,6,7},{8,9,10,11},{12,13,14,15},{32,36,40,44},{33,37,41,4..., dimensions={0} | all-to-all | bytes 1048576 | tf_op jit(solution)/shard_map/all_to_all | solution.py:148
  135.4 0.1 reduce_sum.25
  135.4 6.2 %collective-permute-start.2 = (bf16[64,1024]{1,0:T(8,128)(2,1)S(1)}, bf16[64,1024]{1,0:T(8,128)(2,1)S(1)}, u32[]{:S(2)}, u32[]{:S(2)}) collective-permute-start(bf16[64,1024]{1,0:T(8,128)(2,1)S(1)} %reduce_sum.25), channel_id=1, source_target_pairs={{0,16},{16,0},{1,17},{17,1},{2,18},{18,2},{3,19},{19,3},{4,20},{20... | collective-permute-start | bytes 393224 | tf_op jit(solution)/shard_map/ppermute | solution.py:130
  141.6 13.5 %collective-permute-done.2 = bf16[64,1024]{1,0:T(8,128)(2,1)S(1)} collective-permute-done((bf16[64,1024]{1,0:T(8,128)(2,1)S(1)}, bf16[64,1024]{1,0:T(8,128)(2,1)S(1)}, u32[]{:S(2)}, u32[]{:S(2)}) %collective-permute-start.2) | collective-permute-done | bytes 131104 | tf_op jit(solution)/shard_map/ppermute | solution.py:130
  155.2 0.1 broadcast_in_dim.18
  155.3 9.6 %all_to_all.39 = bf16[4,64,1024]{2,1,0:T(8,128)(2,1)S(1)} all-to-all(bf16[4,64,1024]{2,1,0:T(8,128)(2,1)S(1)} %broadcast_in_dim.18), channel_id=1, replica_groups={{0,1,2,3},{4,5,6,7},{8,9,10,11},{12,13,14,15},{32,36,40,44},{33,37,41,4..., dimensions={0} | all-to-all | bytes 1048576 | tf_op jit(solution)/shard_map/all_to_all | solution.py:148
  164.9 0.3 broadcast_in_dim.19
  165.1 18.1 %all_to_all.40 = bf16[4,4,64,1024]{3,2,1,0:T(8,128)(2,1)S(1)} all-to-all(bf16[4,4,64,1024]{3,2,1,0:T(8,128)(2,1)S(1)} %broadcast_in_dim.19), channel_id=1, replica_groups={{0,4,8,12},{1,5,9,13},{2,6,10,14},{3,7,11,15},{32,33,34,35},{36,37,38,3..., dimensions={0} | all-to-all | bytes 4194304 | tf_op jit(solution)/shard_map/all_to_all | solution.py:148
  183.3 2.6 %bitcast_convert_fusion = f32[1024,1024]{1,0:T(8,128)} fusion(bf16[4,4,64,1024]{3,2,1,0:T(8,128)(2,1)S(1)} %all_to_all.40), kind=kLoop, calls=%fused_computation | loop fusion | flops 1048576 | bytes 6291456 | tf_op jit(solution)/shard_map/convert_element_type | solution.py:208
  (5 shorter events, 0.2 us)
Async XLA Ops:
  0.0 102.5 %copy-start = (bf16[512,1024]{1,0:T(8,128)(2,1)S(1)}, bf16[512,1024]{1,0:T(8,128)(2,1)}, u32[]{:S(2)}) copy-start(bf16[512,1024]{1,0:T(8,128)(2,1)} %param.15) | copy-start | bytes 3145732
  0.0 18.8 %copy-start.1 = (s32[1024]{0:T(1024)S(1)}, s32[1024]{0:T(1024)}, u32[]{:S(2)}) copy-start(s32[1024]{0:T(1024)} %param.13) | copy-start | bytes 12292
  0.0 19.1 %copy-start.2 = (s32[16]{0:T(128)S(1)}, s32[16]{0:T(128)}, u32[]{:S(2)}) copy-start(s32[16]{0:T(128)} %param.14) | copy-start | bytes 196
  2.0 20.6 %collective-permute-start = (bf16[832,256]{1,0:T(8,128)(2,1)S(1)}, bf16[832,256]{1,0:T(8,128)(2,1)}, u32[]{:S(2)}, u32[]{:S(2)}) collective-permute-start(bf16[832,256]{1,0:T(8,128)(2,1)S(1)} %maximum_maximum_fusion), channel_id=1, source_target_pairs={{0,64},{64,0},{1,65},{65,1},{2,66},{66,2},{3,67},{67,3},{4,68},{68... | collective-permute-start | bytes 1277960 | tf_op jit(solution)/shard_map/ppermute | solution.py:130
  7.9 28.6 %all-to-all-start = ((bf16[4,64,512]{2,1,0:T(8,128)(2,1)}), bf16[4,64,512]{2,1,0:T(8,128)(2,1)S(1)}, u32[]{:S(2)}, u32[]{:S(2)}) async-start(bf16[4,64,512]{2,1,0:T(8,128)(2,1)} %broadcast_in_dim.16), calls=%async_computation | async-start | bytes 524288 | tf_op jit(solution)/shard_map/all_to_all | solution.py:28
  91.9 10.4 %collective-permute-start.1 = (bf16[8,64,512]{2,1,0:T(8,128)(2,1)S(1)}, bf16[8,64,512]{2,1,0:T(8,128)(2,1)S(1)}, u32[]{:S(2)}, u32[]{:S(2)}) collective-permute-start(bf16[8,64,512]{2,1,0:T(8,128)(2,1)S(1)} %all_to_all.36), channel_id=1, source_target_pairs={{0,32},{32,0},{1,33},{33,1},{2,34},{34,2},{3,35},{35,3},{4,36},{36... | collective-permute-start | bytes 1572872 | tf_op jit(solution)/shard_map/ppermute | solution.py:130
  135.4 19.7 %collective-permute-start.2 = (bf16[64,1024]{1,0:T(8,128)(2,1)S(1)}, bf16[64,1024]{1,0:T(8,128)(2,1)S(1)}, u32[]{:S(2)}, u32[]{:S(2)}) collective-permute-start(bf16[64,1024]{1,0:T(8,128)(2,1)S(1)} %reduce_sum.25), channel_id=1, source_target_pairs={{0,16},{16,0},{1,17},{17,1},{2,18},{18,2},{3,19},{19,3},{4,20},{20... | collective-permute-start | bytes 393224 | tf_op jit(solution)/shard_map/ppermute | solution.py:130

commit v3 on v2

--- a/solution.py
+++ b/solution.py
@@ -21,11 +21,6 @@
 SCALE = DH**-0.5 * 1.4426950408889634
 BF16 = jnp.bfloat16
 F32 = jnp.float32
-
-
-def sent_to_all(x, axes):
-    copies = jnp.broadcast_to(x, (lax.axis_size(axes), *x.shape))
-    return lax.all_to_all(copies, axes, split_axis=0, concat_axis=0, tiled=True)
 
 
 def attend_kernel(lens_ref, key_pos_ref, query_pos_ref, query_ref, kv_ref, near_kv_ref, out_ref):
@@ -94,7 +89,7 @@
 
 
 def combine_kernel(part_ref, out_ref):
-    width = out_ref.shape[1]
+    width = out_ref.shape[2]
     heads = width // DH
     stats = part_ref[:, :, width:].astype(F32)
     for head in range(heads):
@@ -107,7 +102,8 @@
         scale = scale / jnp.sum(scale * sums, axis=0, keepdims=True)
         columns = slice(head * DH, (head + 1) * DH)
         mixed = jnp.sum(part_ref[:, :, columns].astype(F32) * scale, axis=0)
-        out_ref[:, columns] = mixed.astype(BF16)
+        for copy in range(out_ref.shape[0]):
+            out_ref[copy, :, columns] = mixed.astype(BF16)
 
 
 def combine(parts):
@@ -115,7 +111,7 @@
     vmem = pl.BlockSpec(memory_space=pltpu.VMEM)
     return pl.pallas_call(
         combine_kernel,
-        out_shape=jax.ShapeDtypeStruct((rows, width - DH), BF16),
+        out_shape=jax.ShapeDtypeStruct((lines, rows, width - DH), BF16),
         in_specs=[vmem],
         out_specs=vmem,
         compiler_params=pltpu.CompilerParams(vmem_limit_bytes=8 << 20),
@@ -130,8 +126,56 @@
     return lax.ppermute(x, axis, [(i, i ^ mask) for i in range(lax.axis_size(axis))])
 
 
-def after(x, *others):
-    return lax.optimization_barrier((x, *others))[0]
+def moved_kernel(moves, *refs):
+    *refs, sems = refs
+    started = [
+        pltpu.make_async_copy(source, target, sems.at[i])
+        for i, (source, target) in enumerate(moves(*refs))
+    ]
+    for move in started:
+        move.start()
+    for move in started:
+        move.wait()
+
+
+def moved(moves, count, out_shape, *operands):
+    size = 2 * out_shape.size
+    return pl.pallas_call(
+        functools.partial(moved_kernel, moves),
+        out_shape=out_shape,
+        in_specs=[
+            pl.BlockSpec(memory_space=pltpu.SMEM if x.dtype == jnp.int32 else pl.ANY)
+            for x in operands
+        ],
+        out_specs=pl.BlockSpec(memory_space=pltpu.VMEM),
+        scratch_shapes=[pltpu.SemaphoreType.DMA((count,))],
+        cost_estimate=pl.CostEstimate(flops=0, transcendentals=0, bytes_accessed=2 * size),
+        name="moved",
+    )(*operands)
+
+
+def one_head(column, new_keys, new_values, cache_keys, cache_values):
+    stripe, tokens = cache_keys.shape[0], new_keys.shape[0]
+
+    def moves(column_ref, new_keys_ref, new_values_ref, keys_ref, values_ref, kv_ref):
+        head = pl.ds(pl.multiple_of(column_ref[0], DH), DH)
+        old, new = pl.ds(0, stripe), pl.ds(stripe, tokens)
+        return [
+            (keys_ref.at[:, head], kv_ref.at[old, pl.ds(0, DH)]),
+            (values_ref.at[:, head], kv_ref.at[old, pl.ds(DH, DH)]),
+            (new_keys_ref.at[:, head], kv_ref.at[new, pl.ds(0, DH)]),
+            (new_values_ref.at[:, head], kv_ref.at[new, pl.ds(DH, DH)]),
+        ]
+
+    shape = jax.ShapeDtypeStruct((stripe + tokens, 2 * DH), BF16)
+    return moved(moves, 4, shape, column[None], new_keys, new_values, cache_keys, cache_values)
+
+
+def copied(x, count):
+    def moves(x_ref, out_ref):
+        return [(x_ref, out_ref.at[i]) for i in range(count)]
+
+    return moved(moves, count, jax.ShapeDtypeStruct((count, *x.shape), x.dtype), x)
 
 
 def plane_groups():
@@ -169,16 +213,7 @@
     line, side, core = (lax.axis_index(axis) for axis in SEQ)
     column = lax.axis_index(HEAD) * heads_dev // GQA * DH
 
-    def own(x):
-        return lax.dynamic_slice_in_dim(x, column, DH, 1)
-
-    own_kv = jnp.concatenate(
-        [
-            jnp.concatenate([own(cache_keys), own(new_keys)], axis=0),
-            jnp.concatenate([own(cache_values), own(new_values)], axis=0),
-        ],
-        axis=1,
-    )
+    own_kv = one_head(column, new_keys, new_values, cache_keys, cache_values)
     near_kv = lax.all_gather(swapped(own_kv, NEAR), PAIR)
     kv = lax.all_gather(own_kv, PAIR)
     chips = [line * near + side, line * near + 1 - side]
@@ -194,11 +229,12 @@
     query_pos = lax.dynamic_index_in_dim(
         positions.reshape(lines, near * pair, tok_dev), side * pair + core, 1, keepdims=False
     ).reshape(lines * tok_dev, 1)
-    everyone = sent_to_all(after(queries, own_kv), LINE)
-
+    query, _ = lax.optimization_barrier((queries, own_kv))
+    everyone = lax.all_to_all(copied(query, lines), LINE, 0, 0, tiled=True)
     partial_rows = attend(lens, key_pos, query_pos, everyone, kv, near_kv)
     attended = combine(lax.all_to_all(partial_rows, LINE, 0, 0, tiled=True))
-    attended = joined(sent_to_all(attended, (LINE, NEAR)), PAIR, 1).reshape(-1, width)
+    attended = lax.all_to_all(attended, LINE, 0, 0, tiled=True)
+    attended = joined(joined(attended, NEAR, 1), PAIR, 2).reshape(-1, width)
     partial_out = jnp.dot(attended, out_weight, preferred_element_type=F32).astype(BF16)
     first, second = plane_groups()
     blocks = partial_out.reshape(4, 4, tok_dev, -1)

time: 188 us -> 187 us (level)
  blocking collectives: 113 us -> 104 us
  waiting for transfers between devices: 26.3 us -> 32.6 us
  Pallas kernels: 6.52 us -> 10.2 us
  local copies, waits for them, and re-layouts: 4.19 us -> 0.79 us
  starting transfers between devices: 30.3 us -> 32.3 us
    all_to_all x1, blocking collectives: 26 us -> 17.6 us  [body(): attended = lax.all_to_all(attended, LINE, 0, 0, tiled=True)]
    ppermute x3 -> x4, waiting for transfers between devices: 15 us -> 21.5 us  [swapped(): lax.ppermute(x, axis, [(i, i ^ mask) for i in range(lax.axis_size(axis))])]
    pallas_call x1 -> x3, Pallas kernels: 0.4 us -> 4.04 us  [the longest x2 3.64 us: moved(): pl.pallas_call(functools.partial(moved_kernel, moves), out_shape=out_shap...]
    ppermute x3 -> x4, starting transfers between devices: 19.4 us -> 21.4 us  [swapped(): lax.ppermute(x, axis, [(i, i ^ mask) for i in range(lax.axis_size(axis))])]
  transfers between devices with their start and end apart: 4 -> 5, of which waited for: 3 -> 4; matrix products, arithmetic and copies ran while one was open for 1% -> 0% of each run, Pallas kernels for 0% -> 1%
where the time goes in v3:
time: 187 us; the launch traced here: 186 us
  blocking collectives  104 us (56%)
  waiting for transfers between devices  32.6 us (17%)
  starting transfers between devices  32.3 us (17%)
  Pallas kernels  10.2 us (5%)
  other arithmetic  4.39 us (2%)
    all_to_all x4, blocking collectives, exchanged(): lax.all_to_all(blocks, (PAIR, *PLANE), 0, 0, axis_index_groups=groups, ti...  57.7 us
    all_to_all x1, blocking collectives, body(): attended = combine(lax.all_to_all(partial_rows, LINE, 0, 0, tiled=True))  22.8 us
    ppermute x4, waiting for transfers between devices, swapped(): lax.ppermute(x, axis, [(i, i ^ mask) for i in range(lax.axis_size(axis))])  21.5 us
    ppermute x4, starting transfers between devices, swapped(): lax.ppermute(x, axis, [(i, i ^ mask) for i in range(lax.axis_size(axis))])  21.4 us
    all_to_all x1, blocking collectives, body(): attended = lax.all_to_all(attended, LINE, 0, 0, tiled=True)  17.6 us
    all_to_all x1, waiting for transfers between devices, body(): everyone = lax.all_to_all(copied(query, lines), LINE, 0, 0, tiled=True)  11.1 us
    all_to_all x1, starting transfers between devices, body(): everyone = lax.all_to_all(copied(query, lines), LINE, 0, 0, tiled=True)  10.9 us
    pallas_call x1, Pallas kernels, attend(): pl.pallas_call(attend_kernel, out_shape=jax.ShapeDtypeStruct((lines, rows...  6.12 us
  transfers between devices with their start and end apart: 5, of which 4 were waited for; matrix products, arithmetic and copies ran while one was open for 0% of the time, Pallas kernels for 1%

profile of v3, /device:TPU:1, one launch (start us, length us, event | category | flops | bytes accessed | tf_op | source)
XLA Modules:
  0.0 185.9 jit_solution(3198209985637348705)
XLA Ops:
  0.0 0.0 copy-start
  0.0 0.0 copy-start.1
  0.0 0.0 copy-start.2
  0.0 1.9 %moved.2 = bf16[832,256]{1,0:T(8,128)(2,1)} custom-call(s32[1]{0:T(128)} %bitcast.1.refs_0_, bf16[64,1024]{1,0:T(8,128)(2,1)} %refs_1_.1, bf16[64,1024]{1,0:T(8,128)(2,1)} %refs_2_.1, bf16[768,1024]{1,0:T(8,128)(2,1)} %refs_3_.1, bf16[768,1024]{1,0:T(8,128)(2,1)} %refs_4_.1), custom_call_target="tpu_custom_call" | custom-call | bytes 851968 | tf_op jit(solution)/shard_map/moved/pallas_call | solution.py:143
  1.9 4.4 %collective-permute-start = (bf16[832,256]{1,0:T(8,128)(2,1)}, bf16[832,256]{1,0:T(8,128)(2,1)}, u32[]{:S(2)}, u32[]{:S(2)}) collective-permute-start(bf16[832,256]{1,0:T(8,128)(2,1)} %moved.2), channel_id=1, source_target_pairs={{0,64},{64,0},{1,65},{65,1},{2,66},{66,2},{3,67},{67,3},{4,68},{68... | collective-permute-start | bytes 1277960 | tf_op jit(solution)/shard_map/ppermute | solution.py:126
  6.3 1.7 moved.3
  8.0 10.9 %all-to-all-start = ((bf16[4,64,512]{2,1,0:T(8,128)(2,1)}), bf16[4,64,512]{2,1,0:T(8,128)(2,1)S(1)}, u32[]{:S(2)}, u32[]{:S(2)}) async-start(bf16[4,64,512]{2,1,0:T(8,128)(2,1)} %moved.3), calls=%async_computation | async-start | bytes 524288 | tf_op jit(solution)/shard_map/all_to_all | solution.py:233
  18.9 0.0 copy-done.1
  18.9 0.1 fusion
  19.0 0.1 reshape.16
  19.1 0.1 reshape.23.query_pos_ref
  19.3 0.0 copy-done.2
  19.3 0.1 fusion.1
  19.4 0.1 pad_add_fusion.1.lens_ref
  19.5 3.5 %all-gather = bf16[1664,256]{1,0:T(8,128)(2,1)S(1)} all-gather(bf16[832,256]{1,0:T(8,128)(2,1)} %moved.2), channel_id=2, replica_groups=mesh['line'=4,'near'=2,'core'=2,'far'=2,'x'=4,'y'=4] {'core'}, dimensions={0}, use_global_device_ids=true | all-gather | bytes 1277952 | tf_op jit(solution)/shard_map/all_gather | solution.py:218
  22.9 0.0 collective-permute-done
  22.9 2.6 %all-gather.1 = bf16[1664,256]{1,0:T(8,128)(2,1)S(1)} all-gather(bf16[832,256]{1,0:T(8,128)(2,1)} %collective-permute-done), channel_id=3, replica_groups=mesh['line'=4,'near'=2,'core'=2,'far'=2,'x'=4,'y'=4] {'core'}, dimensions={0}, use_global_device_ids=true | all-gather | bytes 1277952 | tf_op jit(solution)/shard_map/all_gather | solution.py:217
  25.6 11.1 %all-to-all-done.query_ref = bf16[4,64,512]{2,1,0:T(8,128)(2,1)S(1)} async-done(((bf16[4,64,512]{2,1,0:T(8,128)(2,1)}), bf16[4,64,512]{2,1,0:T(8,128)(2,1)S(1)}, u32[]{:S(2)}, u32[]{:S(2)}) %all-to-all-start) | async-done | bytes 262176 | tf_op jit(solution)/shard_map/all_to_all | solution.py:233
  36.6 6.1 %attend.1 = bf16[4,64,640]{2,1,0:T(8,128)(2,1)S(1)} custom-call(s32[4]{0:T(128)S(1)} %pad_add_fusion.1.lens_ref, s32[1,256]{1,0:T(1,128)S(1)} %bitcast.21, s32[256,1]{1,0:T(8,128)S(1)} %reshape.23.query_pos_ref, bf16[4,64,512]{2,1,0:T(8,128)(2,1)S(1)} %all-to-all-done.query_ref, bf16[2,832,256]{2,1,0:T(8,128)(2,1)S(1)} %bitcast.19, ...), custom_call_target="tpu_custom_call" | custom-call | flops 1744830464 | bytes 2228224 | tf_op jit(solution)/shard_map/attend/pallas_call | solution.py:78
  42.8 22.8 %all_to_all.35.part_ref = bf16[4,64,640]{2,1,0:T(8,128)(2,1)S(1)} all-to-all(bf16[4,64,640]{2,1,0:T(8,128)(2,1)S(1)} %attend.1), channel_id=1, replica_groups=mesh['line'=4,'near'=2,'core'=2,'far'=2,'x'=4,'y'=4] {'line'}, dimensions={0} | all-to-all | bytes 655360 | tf_op jit(solution)/shard_map/all_to_all | solution.py:235
  65.6 0.4 combine.1
  66.0 17.6 %all_to_all.36 = bf16[4,64,512]{2,1,0:T(8,128)(2,1)S(1)} all-to-all(bf16[4,64,512]{2,1,0:T(8,128)(2,1)S(1)} %combine.1), channel_id=1, replica_groups=mesh['line'=4,'near'=2,'core'=2,'far'=2,'x'=4,'y'=4] {'line'}, dimensions={0} | all-to-all | bytes 524288 | tf_op jit(solution)/shard_map/all_to_all | solution.py:236
  83.6 1.9 %collective-permute-start.1 = (bf16[4,64,512]{2,1,0:T(8,128)(2,1)S(1)}, bf16[4,64,512]{2,1,0:T(8,128)(2,1)S(1)}, u32[]{:S(2)}, u32[]{:S(2)}) collective-permute-start(bf16[4,64,512]{2,1,0:T(8,128)(2,1)S(1)} %all_to_all.36), channel_id=1, source_target_pairs={{0,64},{64,0},{1,65},{65,1},{2,66},{66,2},{3,67},{67,3},{4,68},{68... | collective-permute-start | bytes 786440 | tf_op jit(solution)/shard_map/ppermute | solution.py:126
  85.5 5.2 %collective-permute-done.1 = bf16[4,64,512]{2,1,0:T(8,128)(2,1)S(1)} collective-permute-done((bf16[4,64,512]{2,1,0:T(8,128)(2,1)S(1)}, bf16[4,64,512]{2,1,0:T(8,128)(2,1)S(1)}, u32[]{:S(2)}, u32[]{:S(2)}) %collective-permute-start.1) | collective-permute-done | bytes 262176 | tf_op jit(solution)/shard_map/ppermute | solution.py:126
  90.7 0.1 pad_maximum_fusion.1
  90.8 6.3 %collective-permute-start.2 = (bf16[4,2,64,512]{3,2,0,1:T(8,128)(2,1)S(1)}, bf16[4,2,64,512]{3,2,0,1:T(8,128)(2,1)S(1)}, u32[]{:S(2)}, u32[]{:S(2)}) collective-permute-start(bf16[4,2,64,512]{3,2,0,1:T(8,128)(2,1)S(1)} %pad_maximum_fusion.1), channel_id=1, source_target_pairs={{0,32},{32,0},{1,33},{33,1},{2,34},{34,2},{3,35},{35,3},{4,36},{36... | collective-permute-start | bytes 1572872 | tf_op jit(solution)/shard_map/ppermute | solution.py:126
  97.1 1.5 collective-permute-done.2
  98.6 0.1 select_bitcast_fusion.1
  98.7 0.1 pad_maximum_fusion
  98.8 0.1 copy.12
  98.9 0.0 copy-done
  98.9 1.3 convolution_convert_fusion
  100.2 19.6 %all_to_all.37 = bf16[4,4,64,1024]{3,2,1,0:T(8,128)(2,1)S(1)} all-to-all(bf16[4,4,64,1024]{3,2,1,0:T(8,128)(2,1)S(1)} %bitcast.22), channel_id=1, replica_groups={{0,4,8,12},{1,5,9,13},{2,6,10,14},{3,7,11,15},{32,33,34,35},{36,37,38,3..., dimensions={0} | all-to-all | bytes 4194304 | tf_op jit(solution)/shard_map/all_to_all | solution.py:192
  119.8 1.3 reduce_sum.24
  121.1 10.7 %all_to_all.38 = bf16[4,64,1024]{2,1,0:T(8,128)(2,1)S(1)} all-to-all(bf16[4,64,1024]{2,1,0:T(8,128)(2,1)} %reduce_sum.24), channel_id=1, replica_groups={{0,1,2,3},{4,5,6,7},{8,9,10,11},{12,13,14,15},{32,36,40,44},{33,37,41,4..., dimensions={0} | all-to-all | bytes 1048576 | tf_op jit(solution)/shard_map/all_to_all | solution.py:192
  131.8 0.1 reduce_sum.25
  131.9 8.8 %collective-permute-start.3 = (bf16[64,1024]{1,0:T(8,128)(2,1)S(1)}, bf16[64,1024]{1,0:T(8,128)(2,1)S(1)}, u32[]{:S(2)}, u32[]{:S(2)}) collective-permute-start(bf16[64,1024]{1,0:T(8,128)(2,1)S(1)} %reduce_sum.25), channel_id=1, source_target_pairs={{0,16},{16,0},{1,17},{17,1},{2,18},{18,2},{3,19},{19,3},{4,20},{20... | collective-permute-start | bytes 393224 | tf_op jit(solution)/shard_map/ppermute | solution.py:126
  140.7 14.8 %collective-permute-done.3 = bf16[64,1024]{1,0:T(8,128)(2,1)S(1)} collective-permute-done((bf16[64,1024]{1,0:T(8,128)(2,1)S(1)}, bf16[64,1024]{1,0:T(8,128)(2,1)S(1)}, u32[]{:S(2)}, u32[]{:S(2)}) %collective-permute-start.3) | collective-permute-done | bytes 131104 | tf_op jit(solution)/shard_map/ppermute | solution.py:126
  155.5 0.1 broadcast_in_dim.14
  155.6 9.3 %all_to_all.39 = bf16[4,64,1024]{2,1,0:T(8,128)(2,1)S(1)} all-to-all(bf16[4,64,1024]{2,1,0:T(8,128)(2,1)S(1)} %broadcast_in_dim.14), channel_id=1, replica_groups={{0,1,2,3},{4,5,6,7},{8,9,10,11},{12,13,14,15},{32,36,40,44},{33,37,41,4..., dimensions={0} | all-to-all | bytes 1048576 | tf_op jit(solution)/shard_map/all_to_all | solution.py:192
  164.9 0.3 broadcast_in_dim.15
  165.2 18.1 %all_to_all.40 = bf16[4,4,64,1024]{3,2,1,0:T(8,128)(2,1)S(1)} all-to-all(bf16[4,4,64,1024]{3,2,1,0:T(8,128)(2,1)S(1)} %broadcast_in_dim.15), channel_id=1, replica_groups={{0,4,8,12},{1,5,9,13},{2,6,10,14},{3,7,11,15},{32,33,34,35},{36,37,38,3..., dimensions={0} | all-to-all | bytes 4194304 | tf_op jit(solution)/shard_map/all_to_all | solution.py:192
  183.3 2.6 %bitcast_convert_fusion = f32[1024,1024]{1,0:T(8,128)} fusion(bf16[4,4,64,1024]{3,2,1,0:T(8,128)(2,1)S(1)} %all_to_all.40), kind=kLoop, calls=%fused_computation | loop fusion | flops 1048576 | bytes 6291456 | tf_op jit(solution)/shard_map/convert_element_type | solution.py:244
  (4 shorter events, 0.1 us)
Async XLA Ops:
  0.0 98.9 %copy-start = (bf16[512,1024]{1,0:T(8,128)(2,1)S(1)}, bf16[512,1024]{1,0:T(8,128)(2,1)}, u32[]{:S(2)}) copy-start(bf16[512,1024]{1,0:T(8,128)(2,1)} %param.15) | copy-start | bytes 3145732
  0.0 18.9 %copy-start.1 = (s32[1024]{0:T(1024)S(1)}, s32[1024]{0:T(1024)}, u32[]{:S(2)}) copy-start(s32[1024]{0:T(1024)} %param.13) | copy-start | bytes 12292
  0.0 19.3 %copy-start.2 = (s32[16]{0:T(128)S(1)}, s32[16]{0:T(128)}, u32[]{:S(2)}) copy-start(s32[16]{0:T(128)} %param.14) | copy-start | bytes 196
  1.9 21.0 %collective-permute-start = (bf16[832,256]{1,0:T(8,128)(2,1)}, bf16[832,256]{1,0:T(8,128)(2,1)}, u32[]{:S(2)}, u32[]{:S(2)}) collective-permute-start(bf16[832,256]{1,0:T(8,128)(2,1)} %moved.2), channel_id=1, source_target_pairs={{0,64},{64,0},{1,65},{65,1},{2,66},{66,2},{3,67},{67,3},{4,68},{68... | collective-permute-start | bytes 1277960 | tf_op jit(solution)/shard_map/ppermute | solution.py:126
  8.0 28.6 %all-to-all-start = ((bf16[4,64,512]{2,1,0:T(8,128)(2,1)}), bf16[4,64,512]{2,1,0:T(8,128)(2,1)S(1)}, u32[]{:S(2)}, u32[]{:S(2)}) async-start(bf16[4,64,512]{2,1,0:T(8,128)(2,1)} %moved.3), calls=%async_computation | async-start | bytes 524288 | tf_op jit(solution)/shard_map/all_to_all | solution.py:233
  83.6 7.1 %collective-permute-start.1 = (bf16[4,64,512]{2,1,0:T(8,128)(2,1)S(1)}, bf16[4,64,512]{2,1,0:T(8,128)(2,1)S(1)}, u32[]{:S(2)}, u32[]{:S(2)}) collective-permute-start(bf16[4,64,512]{2,1,0:T(8,128)(2,1)S(1)} %all_to_all.36), channel_id=1, source_target_pairs={{0,64},{64,0},{1,65},{65,1},{2,66},{66,2},{3,67},{67,3},{4,68},{68... | collective-permute-start | bytes 786440 | tf_op jit(solution)/shard_map/ppermute | solution.py:126
  90.8 7.9 %collective-permute-start.2 = (bf16[4,2,64,512]{3,2,0,1:T(8,128)(2,1)S(1)}, bf16[4,2,64,512]{3,2,0,1:T(8,128)(2,1)S(1)}, u32[]{:S(2)}, u32[]{:S(2)}) collective-permute-start(bf16[4,2,64,512]{3,2,0,1:T(8,128)(2,1)S(1)} %pad_maximum_fusion.1), channel_id=1, source_target_pairs={{0,32},{32,0},{1,33},{33,1},{2,34},{34,2},{3,35},{35,3},{4,36},{36... | collective-permute-start | bytes 1572872 | tf_op jit(solution)/shard_map/ppermute | solution.py:126
  131.9 23.6 %collective-permute-start.3 = (bf16[64,1024]{1,0:T(8,128)(2,1)S(1)}, bf16[64,1024]{1,0:T(8,128)(2,1)S(1)}, u32[]{:S(2)}, u32[]{:S(2)}) collective-permute-start(bf16[64,1024]{1,0:T(8,128)(2,1)S(1)} %reduce_sum.25), channel_id=1, source_target_pairs={{0,16},{16,0},{1,17},{17,1},{2,18},{18,2},{3,19},{19,3},{4,20},{20... | collective-permute-start | bytes 393224 | tf_op jit(solution)/shard_map/ppermute | solution.py:126

commit v4 on v3

--- a/solution.py
+++ b/solution.py
@@ -23,22 +23,42 @@
 F32 = jnp.float32
 
 
-def attend_kernel(lens_ref, key_pos_ref, query_pos_ref, query_ref, kv_ref, near_kv_ref, out_ref):
+def packed(stats):
+    groups = stats.shape[0] // 8
+    return sum(
+        pltpu.roll(stats[8 * i : 8 * (i + 1)], DH // groups * i, 1) for i in range(groups)
+    )
+
+
+def unpacked(tile, rows):
+    groups = rows // 8
+    return jnp.concatenate(
+        [pltpu.roll(tile, (DH - DH // groups * i) % DH, 1) for i in range(groups)], axis=0
+    )
+
+
+def attend_kernel(own, scalars_ref, key_pos_ref, query_pos_ref, query_ref, kv_ref, near_kv_ref, *refs):
+    *own_refs, out_ref = refs
     lines, rows, width = query_ref.shape
     heads = width // DH
-    tokens = lines * rows
     slices = [ref.at[core] for ref in (kv_ref, near_kv_ref) for core in range(2)]
+    line = scalars_ref[len(slices)]
+    taken = [0] if own else [lax.rem(line + i, lines) for i in range(1, lines)]
+    tokens = len(taken) * rows
     stripe = kv_ref.shape[1] - key_pos_ref.shape[1] // len(slices)
     nt = (((1,), (1,)), ((), ()))
     slot = lax.broadcasted_iota(jnp.int32, (1, stripe), 1)
-    live = [slot < lens_ref[i] for i in range(len(slices))]
-    causal = key_pos_ref[...] <= query_pos_ref[...]
+    live = [slot < scalars_ref[i] for i in range(len(slices))]
+    query_pos = jnp.concatenate([query_pos_ref[i] for i in taken], axis=0)
+    causal = key_pos_ref[...] <= query_pos
     new_keys = jnp.concatenate([ref[stripe:, :DH] for ref in slices], axis=0)
     new_values = jnp.concatenate([ref[stripe:, DH:] for ref in slices], axis=0)
+    queries = jnp.concatenate([query_ref[i] for i in taken], axis=0)
     lane = lax.broadcasted_iota(jnp.int32, (tokens, DH), 1)
     stats = jnp.zeros((tokens, DH), F32)
     for head in range(heads):
-        query = query_ref[:, :, head * DH : (head + 1) * DH].reshape(tokens, DH)
+        columns = slice(head * DH, (head + 1) * DH)
+        query = queries[:, columns]
         parts = [
             jnp.where(
                 shown,
@@ -62,56 +82,68 @@
         mixed = sum(
             jnp.dot(part.astype(BF16), value, preferred_element_type=F32)
             for part, value in zip(expo, values)
-        )
-        out_ref[:, :, head * DH : (head + 1) * DH] = mixed.astype(BF16).reshape(lines, rows, DH)
+        ).astype(BF16)
+        for i, block in enumerate(taken):
+            out_ref[block, :rows, columns] = mixed[i * rows : (i + 1) * rows]
         coarse = total.astype(BF16).astype(F32)
         stats = jnp.where(lane == head, peak, stats)
         stats = jnp.where(lane == heads + head, coarse, stats)
         stats = jnp.where(lane == 2 * heads + head, total - coarse, stats)
-    out_ref[:, :, width:] = stats.astype(BF16).reshape(lines, rows, DH)
-
-
-def attend(lens, key_pos, query_pos, queries, kv, near_kv):
+    spare = jnp.zeros((8, width - DH), F32)
+    for i, block in enumerate(taken):
+        tile = jnp.concatenate([packed(stats[i * rows : (i + 1) * rows]), spare], axis=1)
+        out_ref[block, rows:, :] = tile.astype(BF16)
+    for own_ref in own_refs:
+        out_ref[line] = own_ref[0]
+
+
+def attend(scalars, key_pos, query_pos, queries, kv, near_kv, *own_rows):
     lines, rows, width = queries.shape
-    work = lines * rows * (width // DH) * 4 * kv.shape[1]
+    work = max(1, lines - 1) * rows * (width // DH) * 4 * kv.shape[1]
     vmem = pl.BlockSpec(memory_space=pltpu.VMEM)
     return pl.pallas_call(
-        attend_kernel,
-        out_shape=jax.ShapeDtypeStruct((lines, rows, width + DH), BF16),
-        in_specs=[pl.BlockSpec(memory_space=pltpu.SMEM), vmem, vmem, vmem, vmem, vmem],
+        functools.partial(attend_kernel, not own_rows),
+        out_shape=jax.ShapeDtypeStruct((lines, rows + 8, width), BF16),
+        in_specs=[pl.BlockSpec(memory_space=pltpu.SMEM)] + [vmem] * (5 + len(own_rows)),
         out_specs=vmem,
         compiler_params=pltpu.CompilerParams(vmem_limit_bytes=40 << 20),
         cost_estimate=pl.CostEstimate(
             flops=4 * work * DH, transcendentals=work, bytes_accessed=4 * (queries.size + kv.size)
         ),
         name="attend",
-    )(lens, key_pos, query_pos, queries, kv, near_kv)
+    )(scalars, key_pos, query_pos, queries, kv, near_kv, *own_rows)
 
 
 def combine_kernel(part_ref, out_ref):
-    width = out_ref.shape[2]
+    copies, rows, width = out_ref.shape
     heads = width // DH
-    stats = part_ref[:, :, width:].astype(F32)
+    stats = [
+        unpacked(part_ref[i, rows:, :DH].astype(F32), rows) for i in range(part_ref.shape[0])
+    ]
     for head in range(heads):
-        peaks = stats[:, :, head : head + 1]
-        sums = (
-            stats[:, :, heads + head : heads + head + 1]
-            + stats[:, :, 2 * heads + head : 2 * heads + head + 1]
-        )
-        scale = jnp.exp2((peaks - jnp.max(peaks, axis=0, keepdims=True)) * SCALE)
-        scale = scale / jnp.sum(scale * sums, axis=0, keepdims=True)
         columns = slice(head * DH, (head + 1) * DH)
-        mixed = jnp.sum(part_ref[:, :, columns].astype(F32) * scale, axis=0)
-        for copy in range(out_ref.shape[0]):
-            out_ref[copy, :, columns] = mixed.astype(BF16)
+        peaks = [stat[:, head : head + 1] for stat in stats]
+        sums = [
+            stat[:, heads + head : heads + head + 1] + stat[:, 2 * heads + head : 2 * heads + head + 1]
+            for stat in stats
+        ]
+        top = functools.reduce(jnp.maximum, peaks)
+        scales = [jnp.exp2((peak - top) * SCALE) for peak in peaks]
+        inverse = 1.0 / sum(scale * part for scale, part in zip(scales, sums))
+        mixed = sum(
+            part_ref[i, :rows, columns].astype(F32) * (scale * inverse)
+            for i, scale in enumerate(scales)
+        ).astype(BF16)
+        for copy in range(copies):
+            out_ref[copy, :, columns] = mixed
 
 
 def combine(parts):
-    lines, rows, width = parts.shape
+    copies, rows, width = parts.shape
     vmem = pl.BlockSpec(memory_space=pltpu.VMEM)
     return pl.pallas_call(
         combine_kernel,
-        out_shape=jax.ShapeDtypeStruct((lines, rows, width - DH), BF16),
+        out_shape=jax.ShapeDtypeStruct((copies, rows - 8, width), BF16),
         in_specs=[vmem],
         out_specs=vmem,
         compiler_params=pltpu.CompilerParams(vmem_limit_bytes=8 << 20),
@@ -217,8 +249,8 @@
     near_kv = lax.all_gather(swapped(own_kv, NEAR), PAIR)
     kv = lax.all_gather(own_kv, PAIR)
     chips = [line * near + side, line * near + 1 - side]
-    lens = jnp.concatenate(
-        [lax.dynamic_slice_in_dim(cache_len, chip * pair, pair) for chip in chips]
+    scalars = jnp.concatenate(
+        [lax.dynamic_slice_in_dim(cache_len, chip * pair, pair) for chip in chips] + [line[None]]
     )
     key_pos = jnp.concatenate(
         [
@@ -228,10 +260,12 @@
     )[None, :]
     query_pos = lax.dynamic_index_in_dim(
         positions.reshape(lines, near * pair, tok_dev), side * pair + core, 1, keepdims=False
-    ).reshape(lines * tok_dev, 1)
+    )[:, :, None]
     query, _ = lax.optimization_barrier((queries, own_kv))
     everyone = lax.all_to_all(copied(query, lines), LINE, 0, 0, tiled=True)
-    partial_rows = attend(lens, key_pos, query_pos, everyone, kv, near_kv)
+    own_pos = lax.dynamic_slice_in_dim(query_pos, line, 1)
+    own_rows = attend(scalars, key_pos, own_pos, queries[None], kv, near_kv)
+    partial_rows = attend(scalars, key_pos, query_pos, everyone, kv, near_kv, own_rows)
     attended = combine(lax.all_to_all(partial_rows, LINE, 0, 0, tiled=True))
     attended = lax.all_to_all(attended, LINE, 0, 0, tiled=True)
     attended = joined(joined(attended, NEAR, 1), PAIR, 2).reshape(-1, width)

time: 187 us -> 185 us (0.989)
  waiting for transfers between devices: 32.6 us -> 30.3 us
  Pallas kernels: 10.2 us -> 12.4 us
    all_to_all x1, waiting for transfers between devices: 11.1 us -> 7.73 us  [body(): everyone = lax.all_to_all(copied(query, lines), LINE, 0, 0, tiled=True)]
    pallas_call x2 -> x3, Pallas kernels: 6.53 us -> 8.81 us  [the longest x2 8.37 us: attend(): pl.pallas_call(functools.partial(attend_kernel, not own_rows), out_shape=...]
  transfers between devices with their start and end apart: 5 -> 5, of which waited for: 4 -> 4; matrix products, arithmetic and copies ran while one was open for 0% -> 0% of each run, Pallas kernels for 1% -> 3%
where the time goes in v4:
time: 185 us; the launch traced here: 184 us
  blocking collectives  103 us (56%)
  starting transfers between devices  31.7 us (17%)
  waiting for transfers between devices  30.3 us (16%)
  Pallas kernels  12.4 us (7%)
  other arithmetic  4.39 us (2%)
    all_to_all x4, blocking collectives, exchanged(): lax.all_to_all(blocks, (PAIR, *PLANE), 0, 0, axis_index_groups=groups, ti...  57.8 us
    ppermute x4, waiting for transfers between devices, swapped(): lax.ppermute(x, axis, [(i, i ^ mask) for i in range(lax.axis_size(axis))])  22.6 us
    all_to_all x1, blocking collectives, body(): attended = combine(lax.all_to_all(partial_rows, LINE, 0, 0, tiled=True))  21.5 us
    ppermute x4, starting transfers between devices, swapped(): lax.ppermute(x, axis, [(i, i ^ mask) for i in range(lax.axis_size(axis))])  20.8 us
    all_to_all x1, blocking collectives, body(): attended = lax.all_to_all(attended, LINE, 0, 0, tiled=True)  17.1 us
    all_to_all x1, starting transfers between devices, body(): everyone = lax.all_to_all(copied(query, lines), LINE, 0, 0, tiled=True)  10.9 us
    pallas_call x2, Pallas kernels, attend(): pl.pallas_call(functools.partial(attend_kernel, not own_rows), out_shape=...  8.37 us
    all_to_all x1, waiting for transfers between devices, body(): everyone = lax.all_to_all(copied(query, lines), LINE, 0, 0, tiled=True)  7.73 us
  transfers between devices with their start and end apart: 5, of which 4 were waited for; matrix products, arithmetic and copies ran while one was open for 0% of the time, Pallas kernels for 3%

profile of v4, /device:TPU:1, one launch (start us, length us, event | category | flops | bytes accessed | tf_op | source)
XLA Modules:
  0.0 183.7 jit_solution(7371458739819277445)
XLA Ops:
  0.0 0.0 copy-start
  0.0 0.0 copy-start.2
  0.0 0.0 copy-start.3
  0.0 1.9 %moved.2 = bf16[832,256]{1,0:T(8,128)(2,1)} custom-call(s32[1]{0:T(128)} %bitcast.3.refs_0_, bf16[64,1024]{1,0:T(8,128)(2,1)} %refs_1_.1, bf16[64,1024]{1,0:T(8,128)(2,1)} %refs_2_.1, bf16[768,1024]{1,0:T(8,128)(2,1)} %refs_3_.1, bf16[768,1024]{1,0:T(8,128)(2,1)} %refs_4_.1), custom_call_target="tpu_custom_call" | custom-call | bytes 851968 | tf_op jit(solution)/shard_map/moved/pallas_call | solution.py:175
  1.9 0.0 copy-start.1
  1.9 4.5 %collective-permute-start = (bf16[832,256]{1,0:T(8,128)(2,1)}, bf16[832,256]{1,0:T(8,128)(2,1)}, u32[]{:S(2)}, u32[]{:S(2)}) collective-permute-start(bf16[832,256]{1,0:T(8,128)(2,1)} %moved.2), channel_id=1, source_target_pairs={{0,64},{64,0},{1,65},{65,1},{2,66},{66,2},{3,67},{67,3},{4,68},{68... | collective-permute-start | bytes 1277960 | tf_op jit(solution)/shard_map/ppermute | solution.py:158
  6.5 1.7 moved.3
  8.2 10.9 %all-to-all-start = ((bf16[4,64,512]{2,1,0:T(8,128)(2,1)}), bf16[4,64,512]{2,1,0:T(8,128)(2,1)S(1)}, u32[]{:S(2)}, u32[]{:S(2)}) async-start(bf16[4,64,512]{2,1,0:T(8,128)(2,1)} %moved.3), calls=%async_computation | async-start | bytes 524288 | tf_op jit(solution)/shard_map/all_to_all | solution.py:265
  19.1 0.0 copy-done.2
  19.1 0.1 reshape.14
  19.2 0.1 copy.13.query_pos_ref
  19.3 0.1 copy.14.query_pos_ref
  19.4 0.1 fusion
  19.5 0.0 copy-done.3
  19.5 0.1 fusion.1
  19.6 0.1 pad_add_fusion.1.scalars_ref
  19.6 3.5 %all-gather = bf16[1664,256]{1,0:T(8,128)(2,1)S(1)} all-gather(bf16[832,256]{1,0:T(8,128)(2,1)} %moved.2), channel_id=2, replica_groups=mesh['line'=4,'near'=2,'core'=2,'far'=2,'x'=4,'y'=4] {'core'}, dimensions={0}, use_global_device_ids=true | all-gather | bytes 1277952 | tf_op jit(solution)/shard_map/all_gather | solution.py:250
  23.1 0.0 collective-permute-done
  23.1 2.6 %all-gather.1 = bf16[1664,256]{1,0:T(8,128)(2,1)S(1)} all-gather(bf16[832,256]{1,0:T(8,128)(2,1)} %collective-permute-done), channel_id=3, replica_groups=mesh['line'=4,'near'=2,'core'=2,'far'=2,'x'=4,'y'=4] {'core'}, dimensions={0}, use_global_device_ids=true | all-gather | bytes 1277952 | tf_op jit(solution)/shard_map/all_gather | solution.py:249
  25.7 0.0 copy-done.1
  25.7 3.3 %attend.2.refs_0_ = bf16[1,72,512]{2,1,0:T(8,128)(2,1)S(1)} custom-call(s32[5]{0:T(128)S(1)} %pad_add_fusion.1.scalars_ref, s32[1,256]{1,0:T(1,128)S(1)} %bitcast.29, s32[1,64,1]{2,1,0:T(8,128)S(1)} %copy.13.query_pos_ref, bf16[1,64,512]{2,1,0:T(8,128)(2,1)S(1)} %bitcast.28, bf16[2,832,256]{2,1,0:T(8,128)(2,1)S(1)} %bitcast.24, bf16[2,832,256]{2,1,0:T(8,128)(2,1)S(1)} %bitcast.26), custom_call_target="tpu_custom_call" | custom-call | flops 436207616 | bytes 1835008 | tf_op jit(solution)/shard_map/attend/pallas_call | solution.py:104
  29.0 7.7 %all-to-all-done.query_ref = bf16[4,64,512]{2,1,0:T(8,128)(2,1)S(1)} async-done(((bf16[4,64,512]{2,1,0:T(8,128)(2,1)}), bf16[4,64,512]{2,1,0:T(8,128)(2,1)S(1)}, u32[]{:S(2)}, u32[]{:S(2)}) %all-to-all-start) | async-done | bytes 262176 | tf_op jit(solution)/shard_map/all_to_all | solution.py:265
  36.8 5.1 %attend.3 = bf16[4,72,512]{2,1,0:T(8,128)(2,1)S(1)} custom-call(s32[5]{0:T(128)S(1)} %pad_add_fusion.1.scalars_ref, s32[1,256]{1,0:T(1,128)S(1)} %bitcast.30, s32[4,64,1]{2,1,0:T(8,128)S(1)} %copy.14.query_pos_ref, bf16[4,64,512]{2,1,0:T(8,128)(2,1)S(1)} %all-to-all-done.query_ref, bf16[2,832,256]{2,1,0:T(8,128)(2,1)S(1)} %bitcast.25, ...), custom_call_target="tpu_custom_call" | custom-call | flops 1308622848 | bytes 2228224 | tf_op jit(solution)/shard_map/attend/pallas_call | solution.py:104
  41.8 21.5 %all_to_all.35.part_ref = bf16[4,72,512]{2,1,0:T(8,128)(2,1)S(1)} all-to-all(bf16[4,72,512]{2,1,0:T(8,128)(2,1)S(1)} %attend.3), channel_id=1, replica_groups=mesh['line'=4,'near'=2,'core'=2,'far'=2,'x'=4,'y'=4] {'line'}, dimensions={0} | all-to-all | bytes 589824 | tf_op jit(solution)/shard_map/all_to_all | solution.py:269
  63.3 0.4 combine.1
  63.8 17.1 %all_to_all.36 = bf16[4,64,512]{2,1,0:T(8,128)(2,1)S(1)} all-to-all(bf16[4,64,512]{2,1,0:T(8,128)(2,1)S(1)} %combine.1), channel_id=1, replica_groups=mesh['line'=4,'near'=2,'core'=2,'far'=2,'x'=4,'y'=4] {'line'}, dimensions={0} | all-to-all | bytes 524288 | tf_op jit(solution)/shard_map/all_to_all | solution.py:270
  80.9 1.9 %collective-permute-start.1 = (bf16[4,64,512]{2,1,0:T(8,128)(2,1)S(1)}, bf16[4,64,512]{2,1,0:T(8,128)(2,1)S(1)}, u32[]{:S(2)}, u32[]{:S(2)}) collective-permute-start(bf16[4,64,512]{2,1,0:T(8,128)(2,1)S(1)} %all_to_all.36), channel_id=1, source_target_pairs={{0,64},{64,0},{1,65},{65,1},{2,66},{66,2},{3,67},{67,3},{4,68},{68... | collective-permute-start | bytes 786440 | tf_op jit(solution)/shard_map/ppermute | solution.py:158
  82.8 5.2 %collective-permute-done.1 = bf16[4,64,512]{2,1,0:T(8,128)(2,1)S(1)} collective-permute-done((bf16[4,64,512]{2,1,0:T(8,128)(2,1)S(1)}, bf16[4,64,512]{2,1,0:T(8,128)(2,1)S(1)}, u32[]{:S(2)}, u32[]{:S(2)}) %collective-permute-start.1) | collective-permute-done | bytes 262176 | tf_op jit(solution)/shard_map/ppermute | solution.py:158
  88.0 0.1 pad_maximum_fusion.1
  88.1 6.8 %collective-permute-start.2 = (bf16[4,2,64,512]{3,2,0,1:T(8,128)(2,1)S(1)}, bf16[4,2,64,512]{3,2,0,1:T(8,128)(2,1)S(1)}, u32[]{:S(2)}, u32[]{:S(2)}) collective-permute-start(bf16[4,2,64,512]{3,2,0,1:T(8,128)(2,1)S(1)} %pad_maximum_fusion.1), channel_id=1, source_target_pairs={{0,32},{32,0},{1,33},{33,1},{2,34},{34,2},{3,35},{35,3},{4,36},{36... | collective-permute-start | bytes 1572872 | tf_op jit(solution)/shard_map/ppermute | solution.py:158
  94.9 1.5 collective-permute-done.2
  96.4 0.1 select_bitcast_fusion.1
  96.5 0.1 pad_maximum_fusion
  96.6 0.1 copy.15
  96.7 0.0 copy-done
  96.7 1.3 convolution_convert_fusion
  98.0 19.6 %all_to_all.37 = bf16[4,4,64,1024]{3,2,1,0:T(8,128)(2,1)S(1)} all-to-all(bf16[4,4,64,1024]{3,2,1,0:T(8,128)(2,1)S(1)} %bitcast.31), channel_id=1, replica_groups={{0,4,8,12},{1,5,9,13},{2,6,10,14},{3,7,11,15},{32,33,34,35},{36,37,38,3..., dimensions={0} | all-to-all | bytes 4194304 | tf_op jit(solution)/shard_map/all_to_all | solution.py:224
  117.6 1.3 reduce_sum.24
  118.9 10.7 %all_to_all.38 = bf16[4,64,1024]{2,1,0:T(8,128)(2,1)S(1)} all-to-all(bf16[4,64,1024]{2,1,0:T(8,128)(2,1)} %reduce_sum.24), channel_id=1, replica_groups={{0,1,2,3},{4,5,6,7},{8,9,10,11},{12,13,14,15},{32,36,40,44},{33,37,41,4..., dimensions={0} | all-to-all | bytes 1048576 | tf_op jit(solution)/shard_map/all_to_all | solution.py:224
  129.6 0.1 reduce_sum.25
  129.6 7.6 %collective-permute-start.3 = (bf16[64,1024]{1,0:T(8,128)(2,1)S(1)}, bf16[64,1024]{1,0:T(8,128)(2,1)S(1)}, u32[]{:S(2)}, u32[]{:S(2)}) collective-permute-start(bf16[64,1024]{1,0:T(8,128)(2,1)S(1)} %reduce_sum.25), channel_id=1, source_target_pairs={{0,16},{16,0},{1,17},{17,1},{2,18},{18,2},{3,19},{19,3},{4,20},{20... | collective-permute-start | bytes 393224 | tf_op jit(solution)/shard_map/ppermute | solution.py:158
  137.3 15.9 %collective-permute-done.3 = bf16[64,1024]{1,0:T(8,128)(2,1)S(1)} collective-permute-done((bf16[64,1024]{1,0:T(8,128)(2,1)S(1)}, bf16[64,1024]{1,0:T(8,128)(2,1)S(1)}, u32[]{:S(2)}, u32[]{:S(2)}) %collective-permute-start.3) | collective-permute-done | bytes 131104 | tf_op jit(solution)/shard_map/ppermute | solution.py:158
  153.2 0.1 broadcast_in_dim.26
  153.3 9.4 %all_to_all.39 = bf16[4,64,1024]{2,1,0:T(8,128)(2,1)S(1)} all-to-all(bf16[4,64,1024]{2,1,0:T(8,128)(2,1)S(1)} %broadcast_in_dim.26), channel_id=1, replica_groups={{0,1,2,3},{4,5,6,7},{8,9,10,11},{12,13,14,15},{32,36,40,44},{33,37,41,4..., dimensions={0} | all-to-all | bytes 1048576 | tf_op jit(solution)/shard_map/all_to_all | solution.py:224
  162.7 0.3 broadcast_in_dim.27
  162.9 18.1 %all_to_all.40 = bf16[4,4,64,1024]{3,2,1,0:T(8,128)(2,1)S(1)} all-to-all(bf16[4,4,64,1024]{3,2,1,0:T(8,128)(2,1)S(1)} %broadcast_in_dim.27), channel_id=1, replica_groups={{0,4,8,12},{1,5,9,13},{2,6,10,14},{3,7,11,15},{32,33,34,35},{36,37,38,3..., dimensions={0} | all-to-all | bytes 4194304 | tf_op jit(solution)/shard_map/all_to_all | solution.py:224
  181.1 2.6 %bitcast_convert_fusion = f32[1024,1024]{1,0:T(8,128)} fusion(bf16[4,4,64,1024]{3,2,1,0:T(8,128)(2,1)S(1)} %all_to_all.40), kind=kLoop, calls=%fused_computation | loop fusion | flops 1048576 | bytes 6291456 | tf_op jit(solution)/shard_map/convert_element_type | solution.py:278
  (5 shorter events, 0.1 us)
Async XLA Ops:
  0.0 96.7 %copy-start = (bf16[512,1024]{1,0:T(8,128)(2,1)S(1)}, bf16[512,1024]{1,0:T(8,128)(2,1)}, u32[]{:S(2)}) copy-start(bf16[512,1024]{1,0:T(8,128)(2,1)} %param.15) | copy-start | bytes 3145732
  0.0 19.1 %copy-start.2 = (s32[1024]{0:T(1024)S(1)}, s32[1024]{0:T(1024)}, u32[]{:S(2)}) copy-start(s32[1024]{0:T(1024)} %param.13) | copy-start | bytes 12292
  0.0 19.5 %copy-start.3 = (s32[16]{0:T(128)S(1)}, s32[16]{0:T(128)}, u32[]{:S(2)}) copy-start(s32[16]{0:T(128)} %param.14) | copy-start | bytes 196
  1.9 23.8 %copy-start.1 = (bf16[64,512]{1,0:T(8,128)(2,1)S(1)}, bf16[64,512]{1,0:T(8,128)(2,1)}, u32[]{:S(2)}) copy-start(bf16[64,512]{1,0:T(8,128)(2,1)} %refs_0_) | copy-start | bytes 196612
  1.9 21.2 %collective-permute-start = (bf16[832,256]{1,0:T(8,128)(2,1)}, bf16[832,256]{1,0:T(8,128)(2,1)}, u32[]{:S(2)}, u32[]{:S(2)}) collective-permute-start(bf16[832,256]{1,0:T(8,128)(2,1)} %moved.2), channel_id=1, source_target_pairs={{0,64},{64,0},{1,65},{65,1},{2,66},{66,2},{3,67},{67,3},{4,68},{68... | collective-permute-start | bytes 1277960 | tf_op jit(solution)/shard_map/ppermute | solution.py:158
  8.2 28.6 %all-to-all-start = ((bf16[4,64,512]{2,1,0:T(8,128)(2,1)}), bf16[4,64,512]{2,1,0:T(8,128)(2,1)S(1)}, u32[]{:S(2)}, u32[]{:S(2)}) async-start(bf16[4,64,512]{2,1,0:T(8,128)(2,1)} %moved.3), calls=%async_computation | async-start | bytes 524288 | tf_op jit(solution)/shard_map/all_to_all | solution.py:265
  80.9 7.1 %collective-permute-start.1 = (bf16[4,64,512]{2,1,0:T(8,128)(2,1)S(1)}, bf16[4,64,512]{2,1,0:T(8,128)(2,1)S(1)}, u32[]{:S(2)}, u32[]{:S(2)}) collective-permute-start(bf16[4,64,512]{2,1,0:T(8,128)(2,1)S(1)} %all_to_all.36), channel_id=1, source_target_pairs={{0,64},{64,0},{1,65},{65,1},{2,66},{66,2},{3,67},{67,3},{4,68},{68... | collective-permute-start | bytes 786440 | tf_op jit(solution)/shard_map/ppermute | solution.py:158
  88.1 8.3 %collective-permute-start.2 = (bf16[4,2,64,512]{3,2,0,1:T(8,128)(2,1)S(1)}, bf16[4,2,64,512]{3,2,0,1:T(8,128)(2,1)S(1)}, u32[]{:S(2)}, u32[]{:S(2)}) collective-permute-start(bf16[4,2,64,512]{3,2,0,1:T(8,128)(2,1)S(1)} %pad_maximum_fusion.1), channel_id=1, source_target_pairs={{0,32},{32,0},{1,33},{33,1},{2,34},{34,2},{3,35},{35,3},{4,36},{36... | collective-permute-start | bytes 1572872 | tf_op jit(solution)/shard_map/ppermute | solution.py:158
  129.6 23.5 %collective-permute-start.3 = (bf16[64,1024]{1,0:T(8,128)(2,1)S(1)}, bf16[64,1024]{1,0:T(8,128)(2,1)S(1)}, u32[]{:S(2)}, u32[]{:S(2)}) collective-permute-start(bf16[64,1024]{1,0:T(8,128)(2,1)S(1)} %reduce_sum.25), channel_id=1, source_target_pairs={{0,16},{16,0},{1,17},{17,1},{2,18},{18,2},{3,19},{19,3},{4,20},{20... | collective-permute-start | bytes 393224 | tf_op jit(solution)/shard_map/ppermute | solution.py:158

commit v5 on v4

--- a/solution.py
+++ b/solution.py
@@ -210,6 +210,51 @@
     return moved(moves, count, jax.ShapeDtypeStruct((count, *x.shape), x.dtype), x)
 
 
+def widened_kernel(x_ref, out_ref, wide_ref, sems):
+    steps = sems.shape[0]
+    step = x_ref.shape[0] // steps
+    moves = []
+    for i in range(steps):
+        taken = pl.ds(i * step, step)
+        wide_ref[taken, :] = x_ref[taken, :].astype(F32)
+        moves.append(pltpu.make_async_copy(wide_ref.at[taken], out_ref.at[taken], sems.at[i]))
+        moves[-1].start()
+    for move in moves:
+        move.wait()
+
+
+def widened(x, steps=8):
+    return pl.pallas_call(
+        widened_kernel,
+        out_shape=jax.ShapeDtypeStruct(x.shape, F32),
+        in_specs=[pl.BlockSpec(memory_space=pltpu.VMEM)],
+        out_specs=pl.BlockSpec(memory_space=pl.ANY),
+        scratch_shapes=[pltpu.VMEM(x.shape, F32), pltpu.SemaphoreType.DMA((steps,))],
+        compiler_params=pltpu.CompilerParams(vmem_limit_bytes=8 << 20),
+        cost_estimate=pl.CostEstimate(flops=0, transcendentals=0, bytes_accessed=6 * x.size),
+        name="widened",
+    )(x)
+
+
+def summed_kernel(x_ref, out_ref):
+    for block in range(out_ref.shape[0]):
+        total = sum(x_ref[i, block].astype(F32) for i in range(x_ref.shape[0]))
+        out_ref[block] = total.astype(BF16)
+
+
+def summed(x):
+    vmem = pl.BlockSpec(memory_space=pltpu.VMEM)
+    return pl.pallas_call(
+        summed_kernel,
+        out_shape=jax.ShapeDtypeStruct(x.shape[1:], BF16),
+        in_specs=[vmem],
+        out_specs=vmem,
+        compiler_params=pltpu.CompilerParams(vmem_limit_bytes=8 << 20),
+        cost_estimate=pl.CostEstimate(flops=x.size, transcendentals=0, bytes_accessed=3 * x.size),
+        name="summed",
+    )(x)
+
+
 def plane_groups():
     along_x = [[x * 4 + y for x in range(4)] for y in range(4)]
     along_y = [[x * 4 + y for y in range(4)] for x in range(4)]
@@ -272,10 +317,10 @@
     partial_out = jnp.dot(attended, out_weight, preferred_element_type=F32).astype(BF16)
     first, second = plane_groups()
     blocks = partial_out.reshape(4, 4, tok_dev, -1)
-    blocks = summed_on_arrival(summed_on_arrival(blocks, first), second)
+    blocks = summed_on_arrival(summed(exchanged(blocks, first)), second)
     whole = (blocks.astype(F32) + swapped(blocks, FAR).astype(F32)).astype(BF16)
     whole = sent_within(sent_within(whole, second), first)
-    return whole.reshape(partial_out.shape).astype(F32)
+    return widened(whole.reshape(partial_out.shape))
 
 
 def solution(mesh):

time: 185 us -> 183 us (0.989)
  other arithmetic: 4.39 us -> 0.47 us
  Pallas kernels: 12.4 us -> 14.8 us
    convert_element_type x1 -> x0, other arithmetic: 2.61 us -> none  [body(): return whole.reshape(partial_out.shape).astype(F32)]
    pallas_call x0 -> x2, Pallas kernels: none -> 2.36 us  [the longest x1 2.1 us: widened(): pl.pallas_call(widened_kernel, out_shape=jax.ShapeDtypeStruct(x.shape, F3...]
where the time goes in v5:
time: 183 us; the launch traced here: 182 us
  blocking collectives  102 us (56%)
  starting transfers between devices  31.7 us (17%)
  waiting for transfers between devices  30.3 us (17%)
  Pallas kernels  14.8 us (8%)
    all_to_all x4, blocking collectives, exchanged(): lax.all_to_all(blocks, (PAIR, *PLANE), 0, 0, axis_index_groups=groups, ti...  57.6 us
    ppermute x4, waiting for transfers between devices, swapped(): lax.ppermute(x, axis, [(i, i ^ mask) for i in range(lax.axis_size(axis))])  22.6 us
    all_to_all x1, blocking collectives, body(): attended = combine(lax.all_to_all(partial_rows, LINE, 0, 0, tiled=True))  21.5 us
    ppermute x4, starting transfers between devices, swapped(): lax.ppermute(x, axis, [(i, i ^ mask) for i in range(lax.axis_size(axis))])  20.8 us
    all_to_all x1, blocking collectives, body(): attended = lax.all_to_all(attended, LINE, 0, 0, tiled=True)  17.1 us
    all_to_all x1, starting transfers between devices, body(): everyone = lax.all_to_all(copied(query, lines), LINE, 0, 0, tiled=True)  10.9 us
    pallas_call x2, Pallas kernels, attend(): pl.pallas_call(functools.partial(attend_kernel, not own_rows), out_shape=...  8.37 us
    all_to_all x1, waiting for transfers between devices, body(): everyone = lax.all_to_all(copied(query, lines), LINE, 0, 0, tiled=True)  7.72 us
  transfers between devices with their start and end apart: 5, of which 4 were waited for; matrix products, arithmetic and copies ran while one was open for 0% of the time, Pallas kernels for 3%

profile of v5, /device:TPU:1, one launch (start us, length us, event | category | flops | bytes accessed | tf_op | source)
XLA Modules:
  0.0 181.9 jit_solution(1425832995586310858)
XLA Ops:
  0.0 0.0 copy-start
  0.0 0.0 copy-start.2
  0.0 0.0 copy-start.3
  0.0 1.9 %moved.2 = bf16[832,256]{1,0:T(8,128)(2,1)} custom-call(s32[1]{0:T(128)} %bitcast.3.refs_0_, bf16[64,1024]{1,0:T(8,128)(2,1)} %refs_1_.1, bf16[64,1024]{1,0:T(8,128)(2,1)} %refs_2_.1, bf16[768,1024]{1,0:T(8,128)(2,1)} %refs_3_.1, bf16[768,1024]{1,0:T(8,128)(2,1)} %refs_4_.1), custom_call_target="tpu_custom_call" | custom-call | bytes 851968 | tf_op jit(solution)/shard_map/moved/pallas_call | solution.py:175
  1.9 0.0 copy-start.1
  1.9 4.5 %collective-permute-start = (bf16[832,256]{1,0:T(8,128)(2,1)}, bf16[832,256]{1,0:T(8,128)(2,1)}, u32[]{:S(2)}, u32[]{:S(2)}) collective-permute-start(bf16[832,256]{1,0:T(8,128)(2,1)} %moved.2), channel_id=1, source_target_pairs={{0,64},{64,0},{1,65},{65,1},{2,66},{66,2},{3,67},{67,3},{4,68},{68... | collective-permute-start | bytes 1277960 | tf_op jit(solution)/shard_map/ppermute | solution.py:158
  6.5 1.7 moved.3
  8.2 10.9 %all-to-all-start = ((bf16[4,64,512]{2,1,0:T(8,128)(2,1)}), bf16[4,64,512]{2,1,0:T(8,128)(2,1)S(1)}, u32[]{:S(2)}, u32[]{:S(2)}) async-start(bf16[4,64,512]{2,1,0:T(8,128)(2,1)} %moved.3), calls=%async_computation | async-start | bytes 524288 | tf_op jit(solution)/shard_map/all_to_all | solution.py:310
  19.1 0.0 copy-done.2
  19.1 0.1 reshape.14
  19.2 0.1 copy.10.query_pos_ref
  19.3 0.1 copy.11.query_pos_ref
  19.4 0.1 fusion
  19.5 0.0 copy-done.3
  19.5 0.1 fusion.1
  19.5 0.1 pad_add_fusion.1.scalars_ref
  19.6 3.5 %all-gather = bf16[1664,256]{1,0:T(8,128)(2,1)S(1)} all-gather(bf16[832,256]{1,0:T(8,128)(2,1)} %moved.2), channel_id=2, replica_groups=mesh['line'=4,'near'=2,'core'=2,'far'=2,'x'=4,'y'=4] {'core'}, dimensions={0}, use_global_device_ids=true | all-gather | bytes 1277952 | tf_op jit(solution)/shard_map/all_gather | solution.py:295
  23.1 0.0 collective-permute-done
  23.1 2.6 %all-gather.1 = bf16[1664,256]{1,0:T(8,128)(2,1)S(1)} all-gather(bf16[832,256]{1,0:T(8,128)(2,1)} %collective-permute-done), channel_id=3, replica_groups=mesh['line'=4,'near'=2,'core'=2,'far'=2,'x'=4,'y'=4] {'core'}, dimensions={0}, use_global_device_ids=true | all-gather | bytes 1277952 | tf_op jit(solution)/shard_map/all_gather | solution.py:294
  25.7 0.0 copy-done.1
  25.7 3.3 %attend.2.refs_0_ = bf16[1,72,512]{2,1,0:T(8,128)(2,1)S(1)} custom-call(s32[5]{0:T(128)S(1)} %pad_add_fusion.1.scalars_ref, s32[1,256]{1,0:T(1,128)S(1)} %bitcast.28, s32[1,64,1]{2,1,0:T(8,128)S(1)} %copy.10.query_pos_ref, bf16[1,64,512]{2,1,0:T(8,128)(2,1)S(1)} %bitcast.27, bf16[2,832,256]{2,1,0:T(8,128)(2,1)S(1)} %bitcast.23, bf16[2,832,256]{2,1,0:T(8,128)(2,1)S(1)} %bitcast.25), custom_call_target="tpu_custom_call" | custom-call | flops 436207616 | bytes 1835008 | tf_op jit(solution)/shard_map/attend/pallas_call | solution.py:104
  29.0 7.7 %all-to-all-done.query_ref = bf16[4,64,512]{2,1,0:T(8,128)(2,1)S(1)} async-done(((bf16[4,64,512]{2,1,0:T(8,128)(2,1)}), bf16[4,64,512]{2,1,0:T(8,128)(2,1)S(1)}, u32[]{:S(2)}, u32[]{:S(2)}) %all-to-all-start) | async-done | bytes 262176 | tf_op jit(solution)/shard_map/all_to_all | solution.py:310
  36.8 5.1 %attend.3 = bf16[4,72,512]{2,1,0:T(8,128)(2,1)S(1)} custom-call(s32[5]{0:T(128)S(1)} %pad_add_fusion.1.scalars_ref, s32[1,256]{1,0:T(1,128)S(1)} %bitcast.29, s32[4,64,1]{2,1,0:T(8,128)S(1)} %copy.11.query_pos_ref, bf16[4,64,512]{2,1,0:T(8,128)(2,1)S(1)} %all-to-all-done.query_ref, bf16[2,832,256]{2,1,0:T(8,128)(2,1)S(1)} %bitcast.24, ...), custom_call_target="tpu_custom_call" | custom-call | flops 1308622848 | bytes 2228224 | tf_op jit(solution)/shard_map/attend/pallas_call | solution.py:104
  41.8 21.5 %all_to_all.35.part_ref = bf16[4,72,512]{2,1,0:T(8,128)(2,1)S(1)} all-to-all(bf16[4,72,512]{2,1,0:T(8,128)(2,1)S(1)} %attend.3), channel_id=1, replica_groups=mesh['line'=4,'near'=2,'core'=2,'far'=2,'x'=4,'y'=4] {'line'}, dimensions={0} | all-to-all | bytes 589824 | tf_op jit(solution)/shard_map/all_to_all | solution.py:314
  63.3 0.4 combine.1
  63.8 17.1 %all_to_all.36 = bf16[4,64,512]{2,1,0:T(8,128)(2,1)S(1)} all-to-all(bf16[4,64,512]{2,1,0:T(8,128)(2,1)S(1)} %combine.1), channel_id=1, replica_groups=mesh['line'=4,'near'=2,'core'=2,'far'=2,'x'=4,'y'=4] {'line'}, dimensions={0} | all-to-all | bytes 524288 | tf_op jit(solution)/shard_map/all_to_all | solution.py:315
  80.9 1.9 %collective-permute-start.1 = (bf16[4,64,512]{2,1,0:T(8,128)(2,1)S(1)}, bf16[4,64,512]{2,1,0:T(8,128)(2,1)S(1)}, u32[]{:S(2)}, u32[]{:S(2)}) collective-permute-start(bf16[4,64,512]{2,1,0:T(8,128)(2,1)S(1)} %all_to_all.36), channel_id=1, source_target_pairs={{0,64},{64,0},{1,65},{65,1},{2,66},{66,2},{3,67},{67,3},{4,68},{68... | collective-permute-start | bytes 786440 | tf_op jit(solution)/shard_map/ppermute | solution.py:158
  82.8 5.2 %collective-permute-done.1 = bf16[4,64,512]{2,1,0:T(8,128)(2,1)S(1)} collective-permute-done((bf16[4,64,512]{2,1,0:T(8,128)(2,1)S(1)}, bf16[4,64,512]{2,1,0:T(8,128)(2,1)S(1)}, u32[]{:S(2)}, u32[]{:S(2)}) %collective-permute-start.1) | collective-permute-done | bytes 262176 | tf_op jit(solution)/shard_map/ppermute | solution.py:158
  88.0 0.1 pad_maximum_fusion.1
  88.1 6.8 %collective-permute-start.2 = (bf16[4,2,64,512]{3,2,0,1:T(8,128)(2,1)S(1)}, bf16[4,2,64,512]{3,2,0,1:T(8,128)(2,1)S(1)}, u32[]{:S(2)}, u32[]{:S(2)}) collective-permute-start(bf16[4,2,64,512]{3,2,0,1:T(8,128)(2,1)S(1)} %pad_maximum_fusion.1), channel_id=1, source_target_pairs={{0,32},{32,0},{1,33},{33,1},{2,34},{34,2},{3,35},{35,3},{4,36},{36... | collective-permute-start | bytes 1572872 | tf_op jit(solution)/shard_map/ppermute | solution.py:158
  94.9 1.5 collective-permute-done.2
  96.4 0.1 select_bitcast_fusion.1
  96.5 0.1 pad_maximum_fusion
  96.6 0.1 copy.12
  96.7 0.0 copy-done
  96.7 1.3 convolution_convert_fusion
  98.0 19.6 %all_to_all.37.x_ref = bf16[4,4,64,1024]{3,2,1,0:T(8,128)(2,1)S(1)} all-to-all(bf16[4,4,64,1024]{3,2,1,0:T(8,128)(2,1)S(1)} %bitcast.30), channel_id=1, replica_groups={{0,4,8,12},{1,5,9,13},{2,6,10,14},{3,7,11,15},{32,33,34,35},{36,37,38,3..., dimensions={0} | all-to-all | bytes 4194304 | tf_op jit(solution)/shard_map/all_to_all | solution.py:269
  117.6 0.3 summed.1
  117.9 10.4 %all_to_all.38 = bf16[4,64,1024]{2,1,0:T(8,128)(2,1)S(1)} all-to-all(bf16[4,64,1024]{2,1,0:T(8,128)(2,1)S(1)} %summed.1), channel_id=1, replica_groups={{0,1,2,3},{4,5,6,7},{8,9,10,11},{12,13,14,15},{32,36,40,44},{33,37,41,4..., dimensions={0} | all-to-all | bytes 1048576 | tf_op jit(solution)/shard_map/all_to_all | solution.py:269
  128.3 0.1 reduce_sum.12
  128.4 7.6 %collective-permute-start.3 = (bf16[64,1024]{1,0:T(8,128)(2,1)S(1)}, bf16[64,1024]{1,0:T(8,128)(2,1)S(1)}, u32[]{:S(2)}, u32[]{:S(2)}) collective-permute-start(bf16[64,1024]{1,0:T(8,128)(2,1)S(1)} %reduce_sum.12), channel_id=1, source_target_pairs={{0,16},{16,0},{1,17},{17,1},{2,18},{18,2},{3,19},{19,3},{4,20},{20... | collective-permute-start | bytes 393224 | tf_op jit(solution)/shard_map/ppermute | solution.py:158
  136.0 15.9 %collective-permute-done.3 = bf16[64,1024]{1,0:T(8,128)(2,1)S(1)} collective-permute-done((bf16[64,1024]{1,0:T(8,128)(2,1)S(1)}, bf16[64,1024]{1,0:T(8,128)(2,1)S(1)}, u32[]{:S(2)}, u32[]{:S(2)}) %collective-permute-start.3) | collective-permute-done | bytes 131104 | tf_op jit(solution)/shard_map/ppermute | solution.py:158
  151.9 0.1 broadcast_in_dim.26
  152.0 9.4 %all_to_all.39 = bf16[4,64,1024]{2,1,0:T(8,128)(2,1)S(1)} all-to-all(bf16[4,64,1024]{2,1,0:T(8,128)(2,1)S(1)} %broadcast_in_dim.26), channel_id=1, replica_groups={{0,1,2,3},{4,5,6,7},{8,9,10,11},{12,13,14,15},{32,36,40,44},{33,37,41,4..., dimensions={0} | all-to-all | bytes 1048576 | tf_op jit(solution)/shard_map/all_to_all | solution.py:269
  161.4 0.3 broadcast_in_dim.27
  161.7 18.1 %all_to_all.40 = bf16[4,4,64,1024]{3,2,1,0:T(8,128)(2,1)S(1)} all-to-all(bf16[4,4,64,1024]{3,2,1,0:T(8,128)(2,1)S(1)} %broadcast_in_dim.27), channel_id=1, replica_groups={{0,4,8,12},{1,5,9,13},{2,6,10,14},{3,7,11,15},{32,33,34,35},{36,37,38,3..., dimensions={0} | all-to-all | bytes 4194304 | tf_op jit(solution)/shard_map/all_to_all | solution.py:269
  179.8 2.1 %widened.1 = f32[1024,1024]{1,0:T(8,128)} custom-call(bf16[1024,1024]{1,0:T(8,128)(2,1)S(1)} %bitcast.22), custom_call_target="tpu_custom_call" | custom-call | bytes 6291456 | tf_op jit(solution)/shard_map/widened/pallas_call | solution.py:227
  (5 shorter events, 0.1 us)
Async XLA Ops:
  0.0 96.7 %copy-start = (bf16[512,1024]{1,0:T(8,128)(2,1)S(1)}, bf16[512,1024]{1,0:T(8,128)(2,1)}, u32[]{:S(2)}) copy-start(bf16[512,1024]{1,0:T(8,128)(2,1)} %param.15) | copy-start | bytes 3145732
  0.0 19.1 %copy-start.2 = (s32[1024]{0:T(1024)S(1)}, s32[1024]{0:T(1024)}, u32[]{:S(2)}) copy-start(s32[1024]{0:T(1024)} %param.13) | copy-start | bytes 12292
  0.0 19.5 %copy-start.3 = (s32[16]{0:T(128)S(1)}, s32[16]{0:T(128)}, u32[]{:S(2)}) copy-start(s32[16]{0:T(128)} %param.14) | copy-start | bytes 196
  1.9 23.8 %copy-start.1 = (bf16[64,512]{1,0:T(8,128)(2,1)S(1)}, bf16[64,512]{1,0:T(8,128)(2,1)}, u32[]{:S(2)}) copy-start(bf16[64,512]{1,0:T(8,128)(2,1)} %refs_0_) | copy-start | bytes 196612
  1.9 21.2 %collective-permute-start = (bf16[832,256]{1,0:T(8,128)(2,1)}, bf16[832,256]{1,0:T(8,128)(2,1)}, u32[]{:S(2)}, u32[]{:S(2)}) collective-permute-start(bf16[832,256]{1,0:T(8,128)(2,1)} %moved.2), channel_id=1, source_target_pairs={{0,64},{64,0},{1,65},{65,1},{2,66},{66,2},{3,67},{67,3},{4,68},{68... | collective-permute-start | bytes 1277960 | tf_op jit(solution)/shard_map/ppermute | solution.py:158
  8.2 28.6 %all-to-all-start = ((bf16[4,64,512]{2,1,0:T(8,128)(2,1)}), bf16[4,64,512]{2,1,0:T(8,128)(2,1)S(1)}, u32[]{:S(2)}, u32[]{:S(2)}) async-start(bf16[4,64,512]{2,1,0:T(8,128)(2,1)} %moved.3), calls=%async_computation | async-start | bytes 524288 | tf_op jit(solution)/shard_map/all_to_all | solution.py:310
  80.9 7.1 %collective-permute-start.1 = (bf16[4,64,512]{2,1,0:T(8,128)(2,1)S(1)}, bf16[4,64,512]{2,1,0:T(8,128)(2,1)S(1)}, u32[]{:S(2)}, u32[]{:S(2)}) collective-permute-start(bf16[4,64,512]{2,1,0:T(8,128)(2,1)S(1)} %all_to_all.36), channel_id=1, source_target_pairs={{0,64},{64,0},{1,65},{65,1},{2,66},{66,2},{3,67},{67,3},{4,68},{68... | collective-permute-start | bytes 786440 | tf_op jit(solution)/shard_map/ppermute | solution.py:158
  88.1 8.3 %collective-permute-start.2 = (bf16[4,2,64,512]{3,2,0,1:T(8,128)(2,1)S(1)}, bf16[4,2,64,512]{3,2,0,1:T(8,128)(2,1)S(1)}, u32[]{:S(2)}, u32[]{:S(2)}) collective-permute-start(bf16[4,2,64,512]{3,2,0,1:T(8,128)(2,1)S(1)} %pad_maximum_fusion.1), channel_id=1, source_target_pairs={{0,32},{32,0},{1,33},{33,1},{2,34},{34,2},{3,35},{35,3},{4,36},{36... | collective-permute-start | bytes 1572872 | tf_op jit(solution)/shard_map/ppermute | solution.py:158
  128.4 23.5 %collective-permute-start.3 = (bf16[64,1024]{1,0:T(8,128)(2,1)S(1)}, bf16[64,1024]{1,0:T(8,128)(2,1)S(1)}, u32[]{:S(2)}, u32[]{:S(2)}) collective-permute-start(bf16[64,1024]{1,0:T(8,128)(2,1)S(1)} %reduce_sum.12), channel_id=1, source_target_pairs={{0,16},{16,0},{1,17},{17,1},{2,18},{18,2},{3,19},{19,3},{4,20},{20... | collective-permute-start | bytes 393224 | tf_op jit(solution)/shard_map/ppermute | solution.py:158

commit v6 on v5

--- a/solution.py
+++ b/solution.py
@@ -277,10 +277,13 @@
     return exchanged(jnp.broadcast_to(x, (len(groups[0]), *x.shape)), groups)
 
 
-def joined(x, axis, dim):
-    other = swapped(x, axis)
+def ordered(x, other, axis, dim):
     first = lax.axis_index(axis) == 0
     return jnp.stack([jnp.where(first, x, other), jnp.where(first, other, x)], axis=dim)
+
+
+def joined(x, axis, dim):
+    return ordered(x, swapped(x, axis), axis, dim)
 
 
 def body(queries, new_keys, new_values, cache_keys, cache_values, positions, cache_len, out_weight):
@@ -313,7 +316,9 @@
     partial_rows = attend(scalars, key_pos, query_pos, everyone, kv, near_kv, own_rows)
     attended = combine(lax.all_to_all(partial_rows, LINE, 0, 0, tiled=True))
     attended = lax.all_to_all(attended, LINE, 0, 0, tiled=True)
-    attended = joined(joined(attended, NEAR, 1), PAIR, 2).reshape(-1, width)
+    neighbour = swapped(attended, NEAR)
+    attended, neighbour = joined(attended, PAIR, 1), joined(neighbour, PAIR, 1)
+    attended = ordered(attended, neighbour, NEAR, 1).reshape(-1, width)
     partial_out = jnp.dot(attended, out_weight, preferred_element_type=F32).astype(BF16)
     first, second = plane_groups()
     blocks = partial_out.reshape(4, 4, tok_dev, -1)

time: 183 us -> 183 us (level)
  waiting for transfers between devices: 30.3 us -> 24.7 us
  starting transfers between devices: 31.7 us -> 36.9 us
    ppermute x4 -> x5, waiting for transfers between devices: 22.6 us -> 17 us  [swapped(): lax.ppermute(x, axis, [(i, i ^ mask) for i in range(lax.axis_size(axis))])]
    ppermute x4 -> x5, starting transfers between devices: 20.8 us -> 26 us  [swapped(): lax.ppermute(x, axis, [(i, i ^ mask) for i in range(lax.axis_size(axis))])]
  transfers between devices with their start and end apart: 5 -> 6, of which waited for: 4 -> 3; matrix products, arithmetic and copies ran while one was open for 0% -> 0% of each run, Pallas kernels for 3% -> 3%
where the time goes in v6:
time: 183 us; the launch traced here: 182 us
  blocking collectives  102 us (56%)
  starting transfers between devices  36.9 us (20%)
  waiting for transfers between devices  24.7 us (13%)
  Pallas kernels  14.8 us (8%)
    all_to_all x4, blocking collectives, exchanged(): lax.all_to_all(blocks, (PAIR, *PLANE), 0, 0, axis_index_groups=groups, ti...  57.6 us
    ppermute x5, starting transfers between devices, swapped(): lax.ppermute(x, axis, [(i, i ^ mask) for i in range(lax.axis_size(axis))])  26 us
    all_to_all x1, blocking collectives, body(): attended = combine(lax.all_to_all(partial_rows, LINE, 0, 0, tiled=True))  21.5 us
    all_to_all x1, blocking collectives, body(): attended = lax.all_to_all(attended, LINE, 0, 0, tiled=True)  17.1 us
    ppermute x5, waiting for transfers between devices, swapped(): lax.ppermute(x, axis, [(i, i ^ mask) for i in range(lax.axis_size(axis))])  17 us
    all_to_all x1, starting transfers between devices, body(): everyone = lax.all_to_all(copied(query, lines), LINE, 0, 0, tiled=True)  10.9 us
    pallas_call x2, Pallas kernels, attend(): pl.pallas_call(functools.partial(attend_kernel, not own_rows), out_shape=...  8.36 us
    all_to_all x1, waiting for transfers between devices, body(): everyone = lax.all_to_all(copied(query, lines), LINE, 0, 0, tiled=True)  7.73 us
  transfers between devices with their start and end apart: 6, of which 3 were waited for; matrix products, arithmetic and copies ran while one was open for 0% of the time, Pallas kernels for 3%

profile of v6, /device:TPU:1, one launch (start us, length us, event | category | flops | bytes accessed | tf_op | source)
XLA Modules:
  0.0 181.5 jit_solution(3837175554758975363)
XLA Ops:
  0.0 0.0 copy-start
  0.0 0.0 copy-start.2
  0.0 0.0 copy-start.3
  0.0 1.9 %moved.2 = bf16[832,256]{1,0:T(8,128)(2,1)} custom-call(s32[1]{0:T(128)} %bitcast.3.refs_0_, bf16[64,1024]{1,0:T(8,128)(2,1)} %refs_1_.1, bf16[64,1024]{1,0:T(8,128)(2,1)} %refs_2_.1, bf16[768,1024]{1,0:T(8,128)(2,1)} %refs_3_.1, bf16[768,1024]{1,0:T(8,128)(2,1)} %refs_4_.1), custom_call_target="tpu_custom_call" | custom-call | bytes 851968 | tf_op jit(solution)/shard_map/moved/pallas_call | solution.py:175
  1.9 0.0 copy-start.1
  1.9 4.5 %collective-permute-start = (bf16[832,256]{1,0:T(8,128)(2,1)}, bf16[832,256]{1,0:T(8,128)(2,1)}, u32[]{:S(2)}, u32[]{:S(2)}) collective-permute-start(bf16[832,256]{1,0:T(8,128)(2,1)} %moved.2), channel_id=1, source_target_pairs={{0,64},{64,0},{1,65},{65,1},{2,66},{66,2},{3,67},{67,3},{4,68},{68... | collective-permute-start | bytes 1277960 | tf_op jit(solution)/shard_map/ppermute | solution.py:158
  6.5 1.7 moved.3
  8.2 10.9 %all-to-all-start = ((bf16[4,64,512]{2,1,0:T(8,128)(2,1)}), bf16[4,64,512]{2,1,0:T(8,128)(2,1)S(1)}, u32[]{:S(2)}, u32[]{:S(2)}) async-start(bf16[4,64,512]{2,1,0:T(8,128)(2,1)} %moved.3), calls=%async_computation | async-start | bytes 524288 | tf_op jit(solution)/shard_map/all_to_all | solution.py:313
  19.1 0.0 copy-done.2
  19.1 0.1 reshape.132
  19.2 0.1 copy.10.query_pos_ref
  19.3 0.1 copy.11.query_pos_ref
  19.4 0.1 fusion
  19.5 0.0 copy-done.3
  19.5 0.1 fusion.1
  19.6 0.1 pad_add_fusion.1.scalars_ref
  19.6 3.5 %all-gather = bf16[1664,256]{1,0:T(8,128)(2,1)S(1)} all-gather(bf16[832,256]{1,0:T(8,128)(2,1)} %moved.2), channel_id=2, replica_groups=mesh['line'=4,'near'=2,'core'=2,'far'=2,'x'=4,'y'=4] {'core'}, dimensions={0}, use_global_device_ids=true | all-gather | bytes 1277952 | tf_op jit(solution)/shard_map/all_gather | solution.py:298
  23.1 0.0 collective-permute-done
  23.1 2.6 %all-gather.1 = bf16[1664,256]{1,0:T(8,128)(2,1)S(1)} all-gather(bf16[832,256]{1,0:T(8,128)(2,1)} %collective-permute-done), channel_id=3, replica_groups=mesh['line'=4,'near'=2,'core'=2,'far'=2,'x'=4,'y'=4] {'core'}, dimensions={0}, use_global_device_ids=true | all-gather | bytes 1277952 | tf_op jit(solution)/shard_map/all_gather | solution.py:297
  25.7 0.0 copy-done.1
  25.7 3.3 %attend.2.refs_0_ = bf16[1,72,512]{2,1,0:T(8,128)(2,1)S(1)} custom-call(s32[5]{0:T(128)S(1)} %pad_add_fusion.1.scalars_ref, s32[1,256]{1,0:T(1,128)S(1)} %bitcast.28, s32[1,64,1]{2,1,0:T(8,128)S(1)} %copy.10.query_pos_ref, bf16[1,64,512]{2,1,0:T(8,128)(2,1)S(1)} %bitcast.27, bf16[2,832,256]{2,1,0:T(8,128)(2,1)S(1)} %bitcast.23, bf16[2,832,256]{2,1,0:T(8,128)(2,1)S(1)} %bitcast.25), custom_call_target="tpu_custom_call" | custom-call | flops 436207616 | bytes 1835008 | tf_op jit(solution)/shard_map/attend/pallas_call | solution.py:104
  29.0 7.7 %all-to-all-done.query_ref = bf16[4,64,512]{2,1,0:T(8,128)(2,1)S(1)} async-done(((bf16[4,64,512]{2,1,0:T(8,128)(2,1)}), bf16[4,64,512]{2,1,0:T(8,128)(2,1)S(1)}, u32[]{:S(2)}, u32[]{:S(2)}) %all-to-all-start) | async-done | bytes 262176 | tf_op jit(solution)/shard_map/all_to_all | solution.py:313
  36.8 5.1 %attend.3 = bf16[4,72,512]{2,1,0:T(8,128)(2,1)S(1)} custom-call(s32[5]{0:T(128)S(1)} %pad_add_fusion.1.scalars_ref, s32[1,256]{1,0:T(1,128)S(1)} %bitcast.29, s32[4,64,1]{2,1,0:T(8,128)S(1)} %copy.11.query_pos_ref, bf16[4,64,512]{2,1,0:T(8,128)(2,1)S(1)} %all-to-all-done.query_ref, bf16[2,832,256]{2,1,0:T(8,128)(2,1)S(1)} %bitcast.24, ...), custom_call_target="tpu_custom_call" | custom-call | flops 1308622848 | bytes 2228224 | tf_op jit(solution)/shard_map/attend/pallas_call | solution.py:104
  41.8 21.5 %all_to_all.35.part_ref = bf16[4,72,512]{2,1,0:T(8,128)(2,1)S(1)} all-to-all(bf16[4,72,512]{2,1,0:T(8,128)(2,1)S(1)} %attend.3), channel_id=1, replica_groups=mesh['line'=4,'near'=2,'core'=2,'far'=2,'x'=4,'y'=4] {'line'}, dimensions={0} | all-to-all | bytes 589824 | tf_op jit(solution)/shard_map/all_to_all | solution.py:317
  63.3 0.4 combine.1
  63.8 17.1 %all_to_all.36 = bf16[4,64,512]{2,1,0:T(8,128)(2,1)S(1)} all-to-all(bf16[4,64,512]{2,1,0:T(8,128)(2,1)S(1)} %combine.1), channel_id=1, replica_groups=mesh['line'=4,'near'=2,'core'=2,'far'=2,'x'=4,'y'=4] {'line'}, dimensions={0} | all-to-all | bytes 524288 | tf_op jit(solution)/shard_map/all_to_all | solution.py:318
  80.9 1.9 %collective-permute-start.2 = (bf16[4,64,512]{2,1,0:T(8,128)(2,1)S(1)}, bf16[4,64,512]{2,1,0:T(8,128)(2,1)S(1)}, u32[]{:S(2)}, u32[]{:S(2)}) collective-permute-start(bf16[4,64,512]{2,1,0:T(8,128)(2,1)S(1)} %all_to_all.36), channel_id=1, source_target_pairs={{0,64},{64,0},{1,65},{65,1},{2,66},{66,2},{3,67},{67,3},{4,68},{68... | collective-permute-start | bytes 786440 | tf_op jit(solution)/shard_map/ppermute | solution.py:158
  82.8 5.9 %collective-permute-start.1 = (bf16[4,64,512]{2,1,0:T(8,128)(2,1)S(1)}, bf16[4,64,512]{2,1,0:T(8,128)(2,1)S(1)}, u32[]{:S(2)}, u32[]{:S(2)}) collective-permute-start(bf16[4,64,512]{2,1,0:T(8,128)(2,1)S(1)} %all_to_all.36), channel_id=1, source_target_pairs={{0,32},{32,0},{1,33},{33,1},{2,34},{34,2},{3,35},{35,3},{4,36},{36... | collective-permute-start | bytes 786440 | tf_op jit(solution)/shard_map/ppermute | solution.py:158
  88.7 0.0 collective-permute-done.2
  88.7 6.0 %collective-permute-start.3 = (bf16[4,64,512]{2,1,0:T(8,128)(2,1)S(1)}, bf16[4,64,512]{2,1,0:T(8,128)(2,1)S(1)}, u32[]{:S(2)}, u32[]{:S(2)}) collective-permute-start(bf16[4,64,512]{2,1,0:T(8,128)(2,1)S(1)} %collective-permute-done.2), channel_id=1, source_target_pairs={{0,32},{32,0},{1,33},{33,1},{2,34},{34,2},{3,35},{35,3},{4,36},{36... | collective-permute-start | bytes 786440 | tf_op jit(solution)/shard_map/ppermute | solution.py:158
  94.8 0.0 collective-permute-done.1
  94.9 1.1 collective-permute-done.3
  96.0 0.1 broadcast_select_fusion.1
  96.1 0.1 pad_maximum_fusion
  96.2 0.1 copy.12
  96.3 0.0 copy-done
  96.3 1.3 convolution_convert_fusion
  97.5 19.6 %all_to_all.37.x_ref = bf16[4,4,64,1024]{3,2,1,0:T(8,128)(2,1)S(1)} all-to-all(bf16[4,4,64,1024]{3,2,1,0:T(8,128)(2,1)S(1)} %bitcast.30), channel_id=1, replica_groups={{0,4,8,12},{1,5,9,13},{2,6,10,14},{3,7,11,15},{32,33,34,35},{36,37,38,3..., dimensions={0} | all-to-all | bytes 4194304 | tf_op jit(solution)/shard_map/all_to_all | solution.py:269
  117.2 0.3 summed.1
  117.5 10.4 %all_to_all.38 = bf16[4,64,1024]{2,1,0:T(8,128)(2,1)S(1)} all-to-all(bf16[4,64,1024]{2,1,0:T(8,128)(2,1)S(1)} %summed.1), channel_id=1, replica_groups={{0,1,2,3},{4,5,6,7},{8,9,10,11},{12,13,14,15},{32,36,40,44},{33,37,41,4..., dimensions={0} | all-to-all | bytes 1048576 | tf_op jit(solution)/shard_map/all_to_all | solution.py:269
  127.9 0.1 reduce_sum.12
  128.0 7.6 %collective-permute-start.4 = (bf16[64,1024]{1,0:T(8,128)(2,1)S(1)}, bf16[64,1024]{1,0:T(8,128)(2,1)S(1)}, u32[]{:S(2)}, u32[]{:S(2)}) collective-permute-start(bf16[64,1024]{1,0:T(8,128)(2,1)S(1)} %reduce_sum.12), channel_id=1, source_target_pairs={{0,16},{16,0},{1,17},{17,1},{2,18},{18,2},{3,19},{19,3},{4,20},{20... | collective-permute-start | bytes 393224 | tf_op jit(solution)/shard_map/ppermute | solution.py:158
  135.6 15.9 %collective-permute-done.4 = bf16[64,1024]{1,0:T(8,128)(2,1)S(1)} collective-permute-done((bf16[64,1024]{1,0:T(8,128)(2,1)S(1)}, bf16[64,1024]{1,0:T(8,128)(2,1)S(1)}, u32[]{:S(2)}, u32[]{:S(2)}) %collective-permute-start.4) | collective-permute-done | bytes 131104 | tf_op jit(solution)/shard_map/ppermute | solution.py:158
  151.6 0.1 broadcast_in_dim.26
  151.6 9.4 %all_to_all.39 = bf16[4,64,1024]{2,1,0:T(8,128)(2,1)S(1)} all-to-all(bf16[4,64,1024]{2,1,0:T(8,128)(2,1)S(1)} %broadcast_in_dim.26), channel_id=1, replica_groups={{0,1,2,3},{4,5,6,7},{8,9,10,11},{12,13,14,15},{32,36,40,44},{33,37,41,4..., dimensions={0} | all-to-all | bytes 1048576 | tf_op jit(solution)/shard_map/all_to_all | solution.py:269
  161.0 0.3 broadcast_in_dim.27
  161.3 18.1 %all_to_all.40 = bf16[4,4,64,1024]{3,2,1,0:T(8,128)(2,1)S(1)} all-to-all(bf16[4,4,64,1024]{3,2,1,0:T(8,128)(2,1)S(1)} %broadcast_in_dim.27), channel_id=1, replica_groups={{0,4,8,12},{1,5,9,13},{2,6,10,14},{3,7,11,15},{32,33,34,35},{36,37,38,3..., dimensions={0} | all-to-all | bytes 4194304 | tf_op jit(solution)/shard_map/all_to_all | solution.py:269
  179.4 2.1 %widened.1 = f32[1024,1024]{1,0:T(8,128)} custom-call(bf16[1024,1024]{1,0:T(8,128)(2,1)S(1)} %bitcast.22), custom_call_target="tpu_custom_call" | custom-call | bytes 6291456 | tf_op jit(solution)/shard_map/widened/pallas_call | solution.py:227
  (6 shorter events, 0.1 us)
Async XLA Ops:
  0.0 96.3 %copy-start = (bf16[512,1024]{1,0:T(8,128)(2,1)S(1)}, bf16[512,1024]{1,0:T(8,128)(2,1)}, u32[]{:S(2)}) copy-start(bf16[512,1024]{1,0:T(8,128)(2,1)} %param.15) | copy-start | bytes 3145732
  0.0 19.1 %copy-start.2 = (s32[1024]{0:T(1024)S(1)}, s32[1024]{0:T(1024)}, u32[]{:S(2)}) copy-start(s32[1024]{0:T(1024)} %param.13) | copy-start | bytes 12292
  0.0 19.5 %copy-start.3 = (s32[16]{0:T(128)S(1)}, s32[16]{0:T(128)}, u32[]{:S(2)}) copy-start(s32[16]{0:T(128)} %param.14) | copy-start | bytes 196
  1.9 23.8 %copy-start.1 = (bf16[64,512]{1,0:T(8,128)(2,1)S(1)}, bf16[64,512]{1,0:T(8,128)(2,1)}, u32[]{:S(2)}) copy-start(bf16[64,512]{1,0:T(8,128)(2,1)} %refs_0_) | copy-start | bytes 196612
  1.9 21.2 %collective-permute-start = (bf16[832,256]{1,0:T(8,128)(2,1)}, bf16[832,256]{1,0:T(8,128)(2,1)}, u32[]{:S(2)}, u32[]{:S(2)}) collective-permute-start(bf16[832,256]{1,0:T(8,128)(2,1)} %moved.2), channel_id=1, source_target_pairs={{0,64},{64,0},{1,65},{65,1},{2,66},{66,2},{3,67},{67,3},{4,68},{68... | collective-permute-start | bytes 1277960 | tf_op jit(solution)/shard_map/ppermute | solution.py:158
  8.2 28.6 %all-to-all-start = ((bf16[4,64,512]{2,1,0:T(8,128)(2,1)}), bf16[4,64,512]{2,1,0:T(8,128)(2,1)S(1)}, u32[]{:S(2)}, u32[]{:S(2)}) async-start(bf16[4,64,512]{2,1,0:T(8,128)(2,1)} %moved.3), calls=%async_computation | async-start | bytes 524288 | tf_op jit(solution)/shard_map/all_to_all | solution.py:313
  80.9 7.8 %collective-permute-start.2 = (bf16[4,64,512]{2,1,0:T(8,128)(2,1)S(1)}, bf16[4,64,512]{2,1,0:T(8,128)(2,1)S(1)}, u32[]{:S(2)}, u32[]{:S(2)}) collective-permute-start(bf16[4,64,512]{2,1,0:T(8,128)(2,1)S(1)} %all_to_all.36), channel_id=1, source_target_pairs={{0,64},{64,0},{1,65},{65,1},{2,66},{66,2},{3,67},{67,3},{4,68},{68... | collective-permute-start | bytes 786440 | tf_op jit(solution)/shard_map/ppermute | solution.py:158
  82.8 12.0 %collective-permute-start.1 = (bf16[4,64,512]{2,1,0:T(8,128)(2,1)S(1)}, bf16[4,64,512]{2,1,0:T(8,128)(2,1)S(1)}, u32[]{:S(2)}, u32[]{:S(2)}) collective-permute-start(bf16[4,64,512]{2,1,0:T(8,128)(2,1)S(1)} %all_to_all.36), channel_id=1, source_target_pairs={{0,32},{32,0},{1,33},{33,1},{2,34},{34,2},{3,35},{35,3},{4,36},{36... | collective-permute-start | bytes 786440 | tf_op jit(solution)/shard_map/ppermute | solution.py:158
  88.7 7.2 %collective-permute-start.3 = (bf16[4,64,512]{2,1,0:T(8,128)(2,1)S(1)}, bf16[4,64,512]{2,1,0:T(8,128)(2,1)S(1)}, u32[]{:S(2)}, u32[]{:S(2)}) collective-permute-start(bf16[4,64,512]{2,1,0:T(8,128)(2,1)S(1)} %collective-permute-done.2), channel_id=1, source_target_pairs={{0,32},{32,0},{1,33},{33,1},{2,34},{34,2},{3,35},{35,3},{4,36},{36... | collective-permute-start | bytes 786440 | tf_op jit(solution)/shard_map/ppermute | solution.py:158
  128.0 23.5 %collective-permute-start.4 = (bf16[64,1024]{1,0:T(8,128)(2,1)S(1)}, bf16[64,1024]{1,0:T(8,128)(2,1)S(1)}, u32[]{:S(2)}, u32[]{:S(2)}) collective-permute-start(bf16[64,1024]{1,0:T(8,128)(2,1)S(1)} %reduce_sum.12), channel_id=1, source_target_pairs={{0,16},{16,0},{1,17},{17,1},{2,18},{18,2},{3,19},{19,3},{4,20},{20... | collective-permute-start | bytes 393224 | tf_op jit(solution)/shard_map/ppermute | solution.py:158

commit v7 on v6

--- a/solution.py
+++ b/solution.py
@@ -223,7 +223,7 @@
         move.wait()
 
 
-def widened(x, steps=8):
+def widened(x, steps=16):
     return pl.pallas_call(
         widened_kernel,
         out_shape=jax.ShapeDtypeStruct(x.shape, F32),

time: 183 us -> 183 us (level)
  no operation moved by 1% of the time
where the time goes in v7:
time: 183 us; the launch traced here: 182 us
  blocking collectives  102 us (56%)
  starting transfers between devices  36.9 us (20%)
  waiting for transfers between devices  24.7 us (13%)
  Pallas kernels  14.8 us (8%)
    all_to_all x4, blocking collectives, exchanged(): lax.all_to_all(blocks, (PAIR, *PLANE), 0, 0, axis_index_groups=groups, ti...  57.6 us
    ppermute x5, starting transfers between devices, swapped(): lax.ppermute(x, axis, [(i, i ^ mask) for i in range(lax.axis_size(axis))])  26 us
    all_to_all x1, blocking collectives, body(): attended = combine(lax.all_to_all(partial_rows, LINE, 0, 0, tiled=True))  21.5 us
    all_to_all x1, blocking collectives, body(): attended = lax.all_to_all(attended, LINE, 0, 0, tiled=True)  17.1 us
    ppermute x5, waiting for transfers between devices, swapped(): lax.ppermute(x, axis, [(i, i ^ mask) for i in range(lax.axis_size(axis))])  17 us
    all_to_all x1, starting transfers between devices, body(): everyone = lax.all_to_all(copied(query, lines), LINE, 0, 0, tiled=True)  10.9 us
    pallas_call x2, Pallas kernels, attend(): pl.pallas_call(functools.partial(attend_kernel, not own_rows), out_shape=...  8.36 us
    all_to_all x1, waiting for transfers between devices, body(): everyone = lax.all_to_all(copied(query, lines), LINE, 0, 0, tiled=True)  7.73 us
  transfers between devices with their start and end apart: 6, of which 3 were waited for; matrix products, arithmetic and copies ran while one was open for 0% of the time, Pallas kernels for 3%

profile of v7, /device:TPU:1, one launch (start us, length us, event | category | flops | bytes accessed | tf_op | source)
XLA Modules:
  0.0 181.5 jit_solution(14611748012172804966)
XLA Ops:
  0.0 0.0 copy-start
  0.0 0.0 copy-start.2
  0.0 0.0 copy-start.3
  0.0 1.9 %moved.2 = bf16[832,256]{1,0:T(8,128)(2,1)} custom-call(s32[1]{0:T(128)} %bitcast.3.refs_0_, bf16[64,1024]{1,0:T(8,128)(2,1)} %refs_1_.1, bf16[64,1024]{1,0:T(8,128)(2,1)} %refs_2_.1, bf16[768,1024]{1,0:T(8,128)(2,1)} %refs_3_.1, bf16[768,1024]{1,0:T(8,128)(2,1)} %refs_4_.1), custom_call_target="tpu_custom_call" | custom-call | bytes 851968 | tf_op jit(solution)/shard_map/moved/pallas_call | solution.py:175
  1.9 0.0 copy-start.1
  1.9 4.5 %collective-permute-start = (bf16[832,256]{1,0:T(8,128)(2,1)}, bf16[832,256]{1,0:T(8,128)(2,1)}, u32[]{:S(2)}, u32[]{:S(2)}) collective-permute-start(bf16[832,256]{1,0:T(8,128)(2,1)} %moved.2), channel_id=1, source_target_pairs={{0,64},{64,0},{1,65},{65,1},{2,66},{66,2},{3,67},{67,3},{4,68},{68... | collective-permute-start | bytes 1277960 | tf_op jit(solution)/shard_map/ppermute | solution.py:158
  6.5 1.7 moved.3
  8.2 10.9 %all-to-all-start = ((bf16[4,64,512]{2,1,0:T(8,128)(2,1)}), bf16[4,64,512]{2,1,0:T(8,128)(2,1)S(1)}, u32[]{:S(2)}, u32[]{:S(2)}) async-start(bf16[4,64,512]{2,1,0:T(8,128)(2,1)} %moved.3), calls=%async_computation | async-start | bytes 524288 | tf_op jit(solution)/shard_map/all_to_all | solution.py:313
  19.1 0.0 copy-done.2
  19.1 0.1 reshape.132
  19.2 0.1 copy.10.query_pos_ref
  19.3 0.1 copy.11.query_pos_ref
  19.4 0.1 fusion
  19.5 0.0 copy-done.3
  19.5 0.1 fusion.1
  19.6 0.1 pad_add_fusion.1.scalars_ref
  19.6 3.5 %all-gather = bf16[1664,256]{1,0:T(8,128)(2,1)S(1)} all-gather(bf16[832,256]{1,0:T(8,128)(2,1)} %moved.2), channel_id=2, replica_groups=mesh['line'=4,'near'=2,'core'=2,'far'=2,'x'=4,'y'=4] {'core'}, dimensions={0}, use_global_device_ids=true | all-gather | bytes 1277952 | tf_op jit(solution)/shard_map/all_gather | solution.py:298
  23.1 0.0 collective-permute-done
  23.1 2.6 %all-gather.1 = bf16[1664,256]{1,0:T(8,128)(2,1)S(1)} all-gather(bf16[832,256]{1,0:T(8,128)(2,1)} %collective-permute-done), channel_id=3, replica_groups=mesh['line'=4,'near'=2,'core'=2,'far'=2,'x'=4,'y'=4] {'core'}, dimensions={0}, use_global_device_ids=true | all-gather | bytes 1277952 | tf_op jit(solution)/shard_map/all_gather | solution.py:297
  25.7 0.0 copy-done.1
  25.7 3.3 %attend.2.refs_0_ = bf16[1,72,512]{2,1,0:T(8,128)(2,1)S(1)} custom-call(s32[5]{0:T(128)S(1)} %pad_add_fusion.1.scalars_ref, s32[1,256]{1,0:T(1,128)S(1)} %bitcast.28, s32[1,64,1]{2,1,0:T(8,128)S(1)} %copy.10.query_pos_ref, bf16[1,64,512]{2,1,0:T(8,128)(2,1)S(1)} %bitcast.27, bf16[2,832,256]{2,1,0:T(8,128)(2,1)S(1)} %bitcast.23, bf16[2,832,256]{2,1,0:T(8,128)(2,1)S(1)} %bitcast.25), custom_call_target="tpu_custom_call" | custom-call | flops 436207616 | bytes 1835008 | tf_op jit(solution)/shard_map/attend/pallas_call | solution.py:104
  29.0 7.7 %all-to-all-done.query_ref = bf16[4,64,512]{2,1,0:T(8,128)(2,1)S(1)} async-done(((bf16[4,64,512]{2,1,0:T(8,128)(2,1)}), bf16[4,64,512]{2,1,0:T(8,128)(2,1)S(1)}, u32[]{:S(2)}, u32[]{:S(2)}) %all-to-all-start) | async-done | bytes 262176 | tf_op jit(solution)/shard_map/all_to_all | solution.py:313
  36.8 5.1 %attend.3 = bf16[4,72,512]{2,1,0:T(8,128)(2,1)S(1)} custom-call(s32[5]{0:T(128)S(1)} %pad_add_fusion.1.scalars_ref, s32[1,256]{1,0:T(1,128)S(1)} %bitcast.29, s32[4,64,1]{2,1,0:T(8,128)S(1)} %copy.11.query_pos_ref, bf16[4,64,512]{2,1,0:T(8,128)(2,1)S(1)} %all-to-all-done.query_ref, bf16[2,832,256]{2,1,0:T(8,128)(2,1)S(1)} %bitcast.24, ...), custom_call_target="tpu_custom_call" | custom-call | flops 1308622848 | bytes 2228224 | tf_op jit(solution)/shard_map/attend/pallas_call | solution.py:104
  41.8 21.5 %all_to_all.35.part_ref = bf16[4,72,512]{2,1,0:T(8,128)(2,1)S(1)} all-to-all(bf16[4,72,512]{2,1,0:T(8,128)(2,1)S(1)} %attend.3), channel_id=1, replica_groups=mesh['line'=4,'near'=2,'core'=2,'far'=2,'x'=4,'y'=4] {'line'}, dimensions={0} | all-to-all | bytes 589824 | tf_op jit(solution)/shard_map/all_to_all | solution.py:317
  63.3 0.4 combine.1
  63.8 17.1 %all_to_all.36 = bf16[4,64,512]{2,1,0:T(8,128)(2,1)S(1)} all-to-all(bf16[4,64,512]{2,1,0:T(8,128)(2,1)S(1)} %combine.1), channel_id=1, replica_groups=mesh['line'=4,'near'=2,'core'=2,'far'=2,'x'=4,'y'=4] {'line'}, dimensions={0} | all-to-all | bytes 524288 | tf_op jit(solution)/shard_map/all_to_all | solution.py:318
  80.9 1.9 %collective-permute-start.2 = (bf16[4,64,512]{2,1,0:T(8,128)(2,1)S(1)}, bf16[4,64,512]{2,1,0:T(8,128)(2,1)S(1)}, u32[]{:S(2)}, u32[]{:S(2)}) collective-permute-start(bf16[4,64,512]{2,1,0:T(8,128)(2,1)S(1)} %all_to_all.36), channel_id=1, source_target_pairs={{0,64},{64,0},{1,65},{65,1},{2,66},{66,2},{3,67},{67,3},{4,68},{68... | collective-permute-start | bytes 786440 | tf_op jit(solution)/shard_map/ppermute | solution.py:158
  82.8 5.9 %collective-permute-start.1 = (bf16[4,64,512]{2,1,0:T(8,128)(2,1)S(1)}, bf16[4,64,512]{2,1,0:T(8,128)(2,1)S(1)}, u32[]{:S(2)}, u32[]{:S(2)}) collective-permute-start(bf16[4,64,512]{2,1,0:T(8,128)(2,1)S(1)} %all_to_all.36), channel_id=1, source_target_pairs={{0,32},{32,0},{1,33},{33,1},{2,34},{34,2},{3,35},{35,3},{4,36},{36... | collective-permute-start | bytes 786440 | tf_op jit(solution)/shard_map/ppermute | solution.py:158
  88.7 0.0 collective-permute-done.2
  88.7 6.0 %collective-permute-start.3 = (bf16[4,64,512]{2,1,0:T(8,128)(2,1)S(1)}, bf16[4,64,512]{2,1,0:T(8,128)(2,1)S(1)}, u32[]{:S(2)}, u32[]{:S(2)}) collective-permute-start(bf16[4,64,512]{2,1,0:T(8,128)(2,1)S(1)} %collective-permute-done.2), channel_id=1, source_target_pairs={{0,32},{32,0},{1,33},{33,1},{2,34},{34,2},{3,35},{35,3},{4,36},{36... | collective-permute-start | bytes 786440 | tf_op jit(solution)/shard_map/ppermute | solution.py:158
  94.8 0.0 collective-permute-done.1
  94.9 1.1 collective-permute-done.3
  96.0 0.1 broadcast_select_fusion.1
  96.1 0.1 pad_maximum_fusion
  96.2 0.1 copy.12
  96.3 0.0 copy-done
  96.3 1.3 convolution_convert_fusion
  97.5 19.6 %all_to_all.37.x_ref = bf16[4,4,64,1024]{3,2,1,0:T(8,128)(2,1)S(1)} all-to-all(bf16[4,4,64,1024]{3,2,1,0:T(8,128)(2,1)S(1)} %bitcast.30), channel_id=1, replica_groups={{0,4,8,12},{1,5,9,13},{2,6,10,14},{3,7,11,15},{32,33,34,35},{36,37,38,3..., dimensions={0} | all-to-all | bytes 4194304 | tf_op jit(solution)/shard_map/all_to_all | solution.py:269
  117.2 0.3 summed.1
  117.5 10.4 %all_to_all.38 = bf16[4,64,1024]{2,1,0:T(8,128)(2,1)S(1)} all-to-all(bf16[4,64,1024]{2,1,0:T(8,128)(2,1)S(1)} %summed.1), channel_id=1, replica_groups={{0,1,2,3},{4,5,6,7},{8,9,10,11},{12,13,14,15},{32,36,40,44},{33,37,41,4..., dimensions={0} | all-to-all | bytes 1048576 | tf_op jit(solution)/shard_map/all_to_all | solution.py:269
  127.9 0.1 reduce_sum.12
  128.0 7.6 %collective-permute-start.4 = (bf16[64,1024]{1,0:T(8,128)(2,1)S(1)}, bf16[64,1024]{1,0:T(8,128)(2,1)S(1)}, u32[]{:S(2)}, u32[]{:S(2)}) collective-permute-start(bf16[64,1024]{1,0:T(8,128)(2,1)S(1)} %reduce_sum.12), channel_id=1, source_target_pairs={{0,16},{16,0},{1,17},{17,1},{2,18},{18,2},{3,19},{19,3},{4,20},{20... | collective-permute-start | bytes 393224 | tf_op jit(solution)/shard_map/ppermute | solution.py:158
  135.6 15.9 %collective-permute-done.4 = bf16[64,1024]{1,0:T(8,128)(2,1)S(1)} collective-permute-done((bf16[64,1024]{1,0:T(8,128)(2,1)S(1)}, bf16[64,1024]{1,0:T(8,128)(2,1)S(1)}, u32[]{:S(2)}, u32[]{:S(2)}) %collective-permute-start.4) | collective-permute-done | bytes 131104 | tf_op jit(solution)/shard_map/ppermute | solution.py:158
  151.6 0.1 broadcast_in_dim.26
  151.6 9.4 %all_to_all.39 = bf16[4,64,1024]{2,1,0:T(8,128)(2,1)S(1)} all-to-all(bf16[4,64,1024]{2,1,0:T(8,128)(2,1)S(1)} %broadcast_in_dim.26), channel_id=1, replica_groups={{0,1,2,3},{4,5,6,7},{8,9,10,11},{12,13,14,15},{32,36,40,44},{33,37,41,4..., dimensions={0} | all-to-all | bytes 1048576 | tf_op jit(solution)/shard_map/all_to_all | solution.py:269
  161.0 0.3 broadcast_in_dim.27
  161.3 18.1 %all_to_all.40 = bf16[4,4,64,1024]{3,2,1,0:T(8,128)(2,1)S(1)} all-to-all(bf16[4,4,64,1024]{3,2,1,0:T(8,128)(2,1)S(1)} %broadcast_in_dim.27), channel_id=1, replica_groups={{0,4,8,12},{1,5,9,13},{2,6,10,14},{3,7,11,15},{32,33,34,35},{36,37,38,3..., dimensions={0} | all-to-all | bytes 4194304 | tf_op jit(solution)/shard_map/all_to_all | solution.py:269
  179.4 2.1 %widened.1 = f32[1024,1024]{1,0:T(8,128)} custom-call(bf16[1024,1024]{1,0:T(8,128)(2,1)S(1)} %bitcast.22), custom_call_target="tpu_custom_call" | custom-call | bytes 6291456 | tf_op jit(solution)/shard_map/widened/pallas_call | solution.py:227
  (6 shorter events, 0.1 us)
Async XLA Ops:
  0.0 96.3 %copy-start = (bf16[512,1024]{1,0:T(8,128)(2,1)S(1)}, bf16[512,1024]{1,0:T(8,128)(2,1)}, u32[]{:S(2)}) copy-start(bf16[512,1024]{1,0:T(8,128)(2,1)} %param.15) | copy-start | bytes 3145732
  0.0 19.1 %copy-start.2 = (s32[1024]{0:T(1024)S(1)}, s32[1024]{0:T(1024)}, u32[]{:S(2)}) copy-start(s32[1024]{0:T(1024)} %param.13) | copy-start | bytes 12292
  0.0 19.5 %copy-start.3 = (s32[16]{0:T(128)S(1)}, s32[16]{0:T(128)}, u32[]{:S(2)}) copy-start(s32[16]{0:T(128)} %param.14) | copy-start | bytes 196
  1.9 23.8 %copy-start.1 = (bf16[64,512]{1,0:T(8,128)(2,1)S(1)}, bf16[64,512]{1,0:T(8,128)(2,1)}, u32[]{:S(2)}) copy-start(bf16[64,512]{1,0:T(8,128)(2,1)} %refs_0_) | copy-start | bytes 196612
  1.9 21.2 %collective-permute-start = (bf16[832,256]{1,0:T(8,128)(2,1)}, bf16[832,256]{1,0:T(8,128)(2,1)}, u32[]{:S(2)}, u32[]{:S(2)}) collective-permute-start(bf16[832,256]{1,0:T(8,128)(2,1)} %moved.2), channel_id=1, source_target_pairs={{0,64},{64,0},{1,65},{65,1},{2,66},{66,2},{3,67},{67,3},{4,68},{68... | collective-permute-start | bytes 1277960 | tf_op jit(solution)/shard_map/ppermute | solution.py:158
  8.2 28.6 %all-to-all-start = ((bf16[4,64,512]{2,1,0:T(8,128)(2,1)}), bf16[4,64,512]{2,1,0:T(8,128)(2,1)S(1)}, u32[]{:S(2)}, u32[]{:S(2)}) async-start(bf16[4,64,512]{2,1,0:T(8,128)(2,1)} %moved.3), calls=%async_computation | async-start | bytes 524288 | tf_op jit(solution)/shard_map/all_to_all | solution.py:313
  80.9 7.8 %collective-permute-start.2 = (bf16[4,64,512]{2,1,0:T(8,128)(2,1)S(1)}, bf16[4,64,512]{2,1,0:T(8,128)(2,1)S(1)}, u32[]{:S(2)}, u32[]{:S(2)}) collective-permute-start(bf16[4,64,512]{2,1,0:T(8,128)(2,1)S(1)} %all_to_all.36), channel_id=1, source_target_pairs={{0,64},{64,0},{1,65},{65,1},{2,66},{66,2},{3,67},{67,3},{4,68},{68... | collective-permute-start | bytes 786440 | tf_op jit(solution)/shard_map/ppermute | solution.py:158
  82.8 12.0 %collective-permute-start.1 = (bf16[4,64,512]{2,1,0:T(8,128)(2,1)S(1)}, bf16[4,64,512]{2,1,0:T(8,128)(2,1)S(1)}, u32[]{:S(2)}, u32[]{:S(2)}) collective-permute-start(bf16[4,64,512]{2,1,0:T(8,128)(2,1)S(1)} %all_to_all.36), channel_id=1, source_target_pairs={{0,32},{32,0},{1,33},{33,1},{2,34},{34,2},{3,35},{35,3},{4,36},{36... | collective-permute-start | bytes 786440 | tf_op jit(solution)/shard_map/ppermute | solution.py:158
  88.7 7.2 %collective-permute-start.3 = (bf16[4,64,512]{2,1,0:T(8,128)(2,1)S(1)}, bf16[4,64,512]{2,1,0:T(8,128)(2,1)S(1)}, u32[]{:S(2)}, u32[]{:S(2)}) collective-permute-start(bf16[4,64,512]{2,1,0:T(8,128)(2,1)S(1)} %collective-permute-done.2), channel_id=1, source_target_pairs={{0,32},{32,0},{1,33},{33,1},{2,34},{34,2},{3,35},{35,3},{4,36},{36... | collective-permute-start | bytes 786440 | tf_op jit(solution)/shard_map/ppermute | solution.py:158
  128.0 23.5 %collective-permute-start.4 = (bf16[64,1024]{1,0:T(8,128)(2,1)S(1)}, bf16[64,1024]{1,0:T(8,128)(2,1)S(1)}, u32[]{:S(2)}, u32[]{:S(2)}) collective-permute-start(bf16[64,1024]{1,0:T(8,128)(2,1)S(1)} %reduce_sum.12), channel_id=1, source_target_pairs={{0,16},{16,0},{1,17},{17,1},{2,18},{18,2},{3,19},{19,3},{4,20},{20... | collective-permute-start | bytes 393224 | tf_op jit(solution)/shard_map/ppermute | solution.py:158
